TPU v7x, 32 devices: a whole 2x2x4 slice. The times are simulated.
32 devices in a mesh: rep: 4 (over z), exp: 8 (over y, x, core).
Axes of the slice: x: 2, y: 2, z: 4, core: 2. Of those that a mesh axis runs over, the one named last changes fastest.
Arguments:
- tokens: bfloat16 [1536, 2048], P(('rep', 'exp')), may hold values from -6 to 6
- grad_out: bfloat16 [1536, 2048], P(('rep', 'exp')), may hold values from -6 to 6
- expert_ids: int32 [1536, 8], P(('rep', 'exp')), may hold values from 0 to 15, all different within a row; in each aligned block of 48 rows (0 to 47, 48 to 95, ...) at most 26 rows name the same one
- gate_probs: float32 [1536, 8], P(('rep', 'exp')), may hold values from 0.05 to 1
- gate_weight: bfloat16 [32, 2048, 384], P(('rep', 'exp')), may hold values from -0.125 to 0.125
- up_weight: bfloat16 [32, 2048, 384], P(('rep', 'exp')), may hold values from -0.125 to 0.125
- down_weight: bfloat16 [32, 384, 2048], P(('rep', 'exp')), may hold values from -0.21875 to 0.21875
Outputs:
- token_grad: bfloat16 [1536, 2048], P(('rep', 'exp'))
- gate_grad: bfloat16 [32, 2048, 384], P(('rep', 'exp'))
- up_grad: bfloat16 [32, 2048, 384], P(('rep', 'exp'))
- down_grad: bfloat16 [32, 384, 2048], P(('rep', 'exp'))
Inputs may be any that keep to these rules, and one draw needn't show every extreme that they name: `expert_ids`: the 8 experts of a token are distinct; among the 48 tokens of one device no expert is chosen more than 26 times, and that many in some device.
All inputs are finite; a program needn't handle non-finite values.
Results may differ from a plain program's by a relative error of at most 0.0058.
Values may be sent and summed in bfloat16 or wider, within the bound.
No kernel may reach another device: no remote copies, remote signals or barrier semaphores. Data moves between devices by JAX's collectives and lax.ppermute only.
A program may use at most 128 MiB of HBM per device.

v0:
```python
import jax
import jax.numpy as jnp
from jax import lax
from jax.sharding import PartitionSpec as P


def per_device(tokens, grad_out, expert_ids, gate_probs, gate_weight, up_weight, down_weight):
    rep_count = lax.axis_size("rep")
    exp_count = lax.axis_size("exp")
    tok_rows, features = tokens.shape
    top_count = expert_ids.shape[1]
    experts = rep_count * exp_count // 2
    capacity = 2 * ((tok_rows * top_count // experts + 2) // 2)
    routed = tok_rows * top_count
    flat_ids = expert_ids.reshape(routed)
    order_index = jnp.arange(routed, dtype=jnp.int32)
    earlier = (flat_ids[:, None] == flat_ids[None, :]) & (
        order_index[None, :] < order_index[:, None]
    )
    slot_rank = jnp.sum(earlier.astype(jnp.int32), axis=1)
    slot_index = flat_ids * capacity + slot_rank
    slot_range = jnp.arange(experts * capacity, dtype=jnp.int32)
    selector = slot_range[:, None] == slot_index[None, :]
    select_rows = selector.astype(jnp.bfloat16)
    rows_in = jnp.repeat(tokens, top_count, axis=0)
    rows_grad = (
        (gate_probs[:, :, None] * grad_out[:, None, :].astype(jnp.float32))
        .reshape(routed, features)
        .astype(jnp.bfloat16)
    )
    packed_in = jnp.dot(select_rows, rows_in, preferred_element_type=jnp.float32).astype(
        jnp.bfloat16
    )
    packed_grad = jnp.dot(select_rows, rows_grad, preferred_element_type=jnp.float32).astype(
        jnp.bfloat16
    )
    send_in = jnp.repeat(packed_in.reshape(experts, capacity, features), 2, axis=0).reshape(
        rep_count, exp_count, capacity, features
    )
    send_grad = jnp.repeat(packed_grad.reshape(experts, capacity, features), 2, axis=0).reshape(
        rep_count, exp_count, capacity, features
    )
    recv_in, recv_grad = (
        lax.all_to_all(
            lax.all_to_all(send_in, "rep", split_axis=0, concat_axis=0, tiled=True),
            "exp",
            split_axis=1,
            concat_axis=1,
            tiled=True,
        ),
        lax.all_to_all(
            lax.all_to_all(send_grad, "rep", split_axis=0, concat_axis=0, tiled=True),
            "exp",
            split_axis=1,
            concat_axis=1,
            tiled=True,
        ),
    )
    slots = rep_count * exp_count * capacity
    slot_in = recv_in.reshape(slots, features)
    slot_grad = recv_grad.reshape(slots, features)
    gate_mat = gate_weight[0]
    up_mat = up_weight[0]
    down_mat = down_weight[0]
    contract_last = (((1,), (1,)), ((), ()))
    contract_first = (((0,), (0,)), ((), ()))
    gate_pre = jnp.dot(slot_in, gate_mat, preferred_element_type=jnp.float32)
    up_pre = jnp.dot(slot_in, up_mat, preferred_element_type=jnp.float32)
    sigmoid_gate = jax.nn.sigmoid(gate_pre)
    activated = gate_pre * sigmoid_gate
    hidden = (activated * up_pre).astype(jnp.bfloat16)
    hidden_grad = lax.dot_general(
        slot_grad, down_mat, contract_last, preferred_element_type=jnp.float32
    )
    up_in = (hidden_grad * activated).astype(jnp.bfloat16)
    gate_in = (
        hidden_grad * up_pre * sigmoid_gate * (1.0 + gate_pre * (1.0 - sigmoid_gate))
    ).astype(jnp.bfloat16)
    partial_rows = lax.dot_general(
        gate_in, gate_mat, contract_last, preferred_element_type=jnp.float32
    ) + lax.dot_general(up_in, up_mat, contract_last, preferred_element_type=jnp.float32)
    gate_grad = lax.dot_general(
        slot_in, gate_in, contract_first, preferred_element_type=jnp.float32
    ).astype(jnp.bfloat16)[None]
    up_grad = lax.dot_general(
        slot_in, up_in, contract_first, preferred_element_type=jnp.float32
    ).astype(jnp.bfloat16)[None]
    down_grad = lax.dot_general(
        hidden, slot_grad, contract_first, preferred_element_type=jnp.float32
    ).astype(jnp.bfloat16)[None]
    partial_grid = partial_rows.reshape(rep_count, exp_count, capacity, features)
    returned_grid = lax.all_to_all(
        lax.all_to_all(partial_grid, "rep", split_axis=0, concat_axis=0, tiled=True),
        "exp",
        split_axis=1,
        concat_axis=1,
        tiled=True,
    )
    returned = jnp.sum(returned_grid.reshape(experts, 2, capacity, features), axis=1).reshape(
        experts * capacity, features
    )
    routed_grads = returned[slot_index]
    token_grad = jnp.sum(routed_grads.reshape(tok_rows, top_count, features), axis=1).astype(
        jnp.bfloat16
    )
    return (token_grad, gate_grad, up_grad, down_grad)


def solution(mesh):
    return jax.shard_map(
        per_device,
        mesh=mesh,
        in_specs=(
            P(("rep", "exp"), None),
            P(("rep", "exp"), None),
            P(("rep", "exp"), None),
            P(("rep", "exp"), None),
            P(("rep", "exp"), None, None),
            P(("rep", "exp"), None, None),
            P(("rep", "exp"), None, None),
        ),
        out_specs=(
            P(("rep", "exp"), None),
            P(("rep", "exp"), None, None),
            P(("rep", "exp"), None, None),
            P(("rep", "exp"), None, None),
        ),
        check_vma=False,
    )
```

profile of v0, /device:TPU:0, one launch (start us, length us, event | category | flops | bytes accessed | tf_op | source)
XLA Modules:
  0.0 607.8 jit_solution(6610514877858975886)
XLA Ops:
  0.6 0.0 copy-start
  0.6 0.9 copy.52
  1.5 0.1 reshape.83
  1.6 0.2 convert_reduce_fusion
  1.9 2.0 convolution_convert_fusion
  3.8 1.6 reshape.87
  5.5 2.5 copy.58
  8.0 3.4 broadcast_in_dim.27
  11.4 8.2 %reshape_reshape.7 = bf16[4,8,26,2048]{3,1,0,2:T(8,128)(2,1)} reshape(bf16[16,2,26,2048]{3,1,0,2:T(2,128)(2,1)} %broadcast_in_dim.27) | data formatting | bytes 6815744 | tf_op jit(solution)/shard_map/reshape;reshape | solution.py:37
  19.5 4.2 copy.59
  23.7 6.5 %all-to-all-start.2 = ((bf16[4,8,26,2048]{3,1,2,0:T(8,128)(2,1)}), bf16[4,8,26,2048]{3,1,2,0:T(8,128)(2,1)}, u32[]{:S(2)}, u32[]{:S(2)}) async-start(bf16[4,8,26,2048]{3,1,2,0:T(8,128)(2,1)} %copy.59), calls=%async_computation.2 | async-start | bytes 6815744 | tf_op jit(solution)/shard_map/all_to_all | solution.py:45
  30.2 0.0 copy-done.12
  30.2 0.1 copy.53
  30.3 0.1 mul.65
  30.4 1.2 convolution_convert_fusion.1
  31.6 1.7 reshape.84
  33.2 2.5 copy.54
  35.8 3.4 broadcast_in_dim.12
  39.2 8.2 %reshape_reshape.6 = bf16[4,8,26,2048]{3,1,0,2:T(8,128)(2,1)} reshape(bf16[16,2,26,2048]{3,1,0,2:T(2,128)(2,1)} %broadcast_in_dim.12) | data formatting | bytes 6815744 | tf_op jit(solution)/shard_map/reshape;reshape | solution.py:40
  47.3 4.3 copy.55
  51.6 55.0 %all-to-all-done.2 = bf16[4,8,26,2048]{3,1,2,0:T(8,128)(2,1)} async-done(((bf16[4,8,26,2048]{3,1,2,0:T(8,128)(2,1)}), bf16[4,8,26,2048]{3,1,2,0:T(8,128)(2,1)}, u32[]{:S(2)}, u32[]{:S(2)}) %all-to-all-start.2) | async-done | bytes 3407904 | tf_op jit(solution)/shard_map/all_to_all | solution.py:45
  106.6 4.8 all-to-all-start
  111.4 6.3 %copy.60 = bf16[4,8,26,2048]{3,0,2,1:T(4,128)(2,1)} copy(bf16[4,8,26,2048]{3,1,2,0:T(8,128)(2,1)} %all-to-all-done.2) | data formatting | bytes 6815744 | tf_op jit(solution)/shard_map/all_to_all | solution.py:45
  117.7 69.5 %all-to-all-done = bf16[4,8,26,2048]{3,1,2,0:T(8,128)(2,1)} async-done(((bf16[4,8,26,2048]{3,1,2,0:T(8,128)(2,1)}), bf16[4,8,26,2048]{3,1,2,0:T(8,128)(2,1)}, u32[]{:S(2)}, u32[]{:S(2)}) %all-to-all-start) | async-done | bytes 3407904 | tf_op jit(solution)/shard_map/all_to_all | solution.py:52
  187.2 4.9 all-to-all-start.3
  192.1 6.3 %copy.56 = bf16[4,8,26,2048]{3,0,2,1:T(4,128)(2,1)} copy(bf16[4,8,26,2048]{3,1,2,0:T(8,128)(2,1)} %all-to-all-done) | data formatting | bytes 6815744 | tf_op jit(solution)/shard_map/all_to_all | solution.py:52
  198.5 34.3 %all-to-all-done.3 = bf16[4,8,26,2048]{3,0,2,1:T(4,128)(2,1)} async-done(((bf16[4,8,26,2048]{3,0,2,1:T(4,128)(2,1)}), bf16[4,8,26,2048]{3,0,2,1:T(4,128)(2,1)}, u32[]{:S(2)}, u32[]{:S(2)}) %all-to-all-start.3) | async-done | bytes 3407904 | tf_op jit(solution)/shard_map/all_to_all | solution.py:44
  232.8 4.5 all-to-all-start.1
  237.3 5.9 copy.61
  243.1 4.9 reshape.88
  248.1 5.1 fusion.7
  253.2 3.0 fusion.10
  256.2 21.8 %all-to-all-done.1 = bf16[4,8,26,2048]{3,0,2,1:T(4,128)(2,1)} async-done(((bf16[4,8,26,2048]{3,0,2,1:T(4,128)(2,1)}), bf16[4,8,26,2048]{3,0,2,1:T(4,128)(2,1)}, u32[]{:S(2)}, u32[]{:S(2)}) %all-to-all-start.1) | async-done | bytes 3407904 | tf_op jit(solution)/shard_map/all_to_all | solution.py:51
  278.0 5.9 copy.57
  283.8 4.9 reshape.85
  288.7 5.4 multiply_convert_fusion.1
  294.1 0.0 copy-start.6
  294.1 0.0 copy-start.8
  294.2 2.0 fusion.5
  296.1 0.0 copy-done.6
  296.1 0.0 copy-done.8
  296.1 4.8 convolution_add_fusion
  301.0 6.9 %reshape.89 = f32[4,8,26,2048]{3,2,1,0:T(8,128)} reshape(f32[832,2048]{1,0:T(8,128)} %convolution_add_fusion) | data formatting | bytes 13631488 | tf_op jit(solution)/shard_map/reshape | solution.py:91
  307.8 7.3 %copy.62 = f32[4,8,26,2048]{3,1,2,0:T(8,128)S(1)} copy(f32[4,8,26,2048]{3,2,1,0:T(8,128)} %reshape.89) | data formatting | bytes 13631488 | tf_op jit(solution)/shard_map/reshape | solution.py:91
  315.2 149.3 %all_to_all.30 = f32[4,8,26,2048]{3,1,2,0:T(8,128)S(1)} all-to-all(f32[4,8,26,2048]{3,1,2,0:T(8,128)S(1)} %copy.62), channel_id=1, replica_groups=mesh['rep'=4,'exp'=8] {'rep'}, dimensions={0} | all-to-all | bytes 13631488 | tf_op jit(solution)/shard_map/all_to_all | solution.py:93
  464.5 7.3 %copy.63 = f32[4,8,26,2048]{3,0,2,1:T(4,128)} copy(f32[4,8,26,2048]{3,1,2,0:T(8,128)S(1)} %all_to_all.30) | data formatting | bytes 13631488 | tf_op jit(solution)/shard_map/all_to_all | solution.py:93
  471.8 5.3 all-to-all-start.5
  477.1 0.1 copy.66
  477.1 0.1 mul.78
  477.3 0.0 copy-done.9
  477.3 0.0 copy-start.3
  477.3 0.0 copy-start.7
  477.3 5.5 fusion.2
  482.9 3.5 fusion.1
  486.3 0.0 copy-done.14
  486.3 3.1 fusion.3
  489.4 64.7 %all-to-all-done.5 = f32[4,8,26,2048]{3,0,2,1:T(4,128)} async-done(((f32[4,8,26,2048]{3,0,2,1:T(4,128)}), f32[4,8,26,2048]{3,0,2,1:T(4,128)}, u32[]{:S(2)}, u32[]{:S(2)}) %all-to-all-start.5) | async-done | bytes 6815776 | tf_op jit(solution)/shard_map/all_to_all | solution.py:92
  554.1 12.1 %copy.64 = f32[4,8,26,2048]{3,1,0,2:T(8,128)} copy(f32[4,8,26,2048]{3,0,2,1:T(4,128)} %all-to-all-done.5) | data formatting | bytes 13631488 | tf_op jit(solution)/shard_map/all_to_all | solution.py:92
  566.2 9.0 %reshape.90 = f32[16,2,26,2048]{3,1,0,2:T(2,128)} reshape(f32[4,8,26,2048]{3,1,0,2:T(8,128)} %copy.64) | data formatting | bytes 13631488 | tf_op jit(solution)/shard_map/reshape | solution.py:99
  575.3 12.0 %reduce_sum.30 = f32[16,26,2048]{2,0,1:T(8,128)} reduce(f32[16,2,26,2048]{3,1,0,2:T(2,128)} %reshape.90, f32[]{:T(128)} %constant.2.clone.1), dimensions={1}, to_apply=%region_1.0 | reduce | flops 851968 | bytes 10223620 | tf_op jit(solution)/shard_map/reduce_sum | solution.py:99
  587.3 5.9 copy.65
  593.2 3.6 reshape.91
  596.9 7.1 %gather_fusion = f32[384,2048]{1,0:T(8,128)} fusion(f32[416,2048]{1,0:T(8,128)} %reshape.91, s32[1024]{0:T(1024)S(1)} %pad_clamp_fusion), kind=kCustom, calls=%fused_computation | custom fusion | bytes 6292992 | tf_op jit(solution)/shard_map/gather | solution.py:102
  604.0 3.3 bitcast_reduce_fusion
  (25 shorter events, 0.1 us)
Async XLA Ops:
  0.6 247.4 %copy-start = (bf16[1,2048,384]{2,1,0:T(8,128)(2,1)S(1)}, bf16[1,2048,384]{2,1,0:T(8,128)(2,1)}, u32[]{:S(2)}) copy-start(bf16[1,2048,384]{2,1,0:T(8,128)(2,1)} %param.11) | copy-start | bytes 4718596
  23.7 6.5 %copy-start.12 = (f32[48,8]{0,1:T(8,128)S(1)}, f32[48,8]{0,1:T(8,128)}, u32[]{:S(2)}) copy-start(f32[48,8]{0,1:T(8,128)} %param.10) | copy-start | bytes 4612
  23.7 6.7 %copy-start.10 = (bf16[48,2048]{1,0:T(8,128)(2,1)S(1)}, bf16[48,2048]{1,0:T(8,128)(2,1)}, u32[]{:S(2)}) copy-start(bf16[48,2048]{1,0:T(8,128)(2,1)} %param.8) | copy-start | bytes 589828
  23.7 82.9 %all-to-all-start.2 = ((bf16[4,8,26,2048]{3,1,2,0:T(8,128)(2,1)}), bf16[4,8,26,2048]{3,1,2,0:T(8,128)(2,1)}, u32[]{:S(2)}, u32[]{:S(2)}) async-start(bf16[4,8,26,2048]{3,1,2,0:T(8,128)(2,1)} %copy.59), calls=%async_computation.2 | async-start | bytes 6815744 | tf_op jit(solution)/shard_map/all_to_all | solution.py:45
  106.6 80.6 %all-to-all-start = ((bf16[4,8,26,2048]{3,1,2,0:T(8,128)(2,1)}), bf16[4,8,26,2048]{3,1,2,0:T(8,128)(2,1)}, u32[]{:S(2)}, u32[]{:S(2)}) async-start(bf16[4,8,26,2048]{3,1,2,0:T(8,128)(2,1)} %copy.55), calls=%async_computation | async-start | bytes 6815744 | tf_op jit(solution)/shard_map/all_to_all | solution.py:52
  187.2 45.6 %all-to-all-start.3 = ((bf16[4,8,26,2048]{3,0,2,1:T(4,128)(2,1)}), bf16[4,8,26,2048]{3,0,2,1:T(4,128)(2,1)}, u32[]{:S(2)}, u32[]{:S(2)}) async-start(bf16[4,8,26,2048]{3,0,2,1:T(4,128)(2,1)} %copy.60), calls=%async_computation.3 | async-start | bytes 6815744 | tf_op jit(solution)/shard_map/all_to_all | solution.py:44
  232.8 45.2 %all-to-all-start.1 = ((bf16[4,8,26,2048]{3,0,2,1:T(4,128)(2,1)}), bf16[4,8,26,2048]{3,0,2,1:T(4,128)(2,1)}, u32[]{:S(2)}, u32[]{:S(2)}) async-start(bf16[4,8,26,2048]{3,0,2,1:T(4,128)(2,1)} %copy.56), calls=%async_computation.1 | async-start | bytes 6815744 | tf_op jit(solution)/shard_map/all_to_all | solution.py:51
  248.1 5.1 copy-start.2
  248.1 5.1 copy-start.5
  294.1 2.0 copy-start.6
  294.1 2.0 copy-start.8
  471.8 5.3 copy-start.11
  471.8 5.5 copy-start.9
  471.8 82.4 %all-to-all-start.5 = ((f32[4,8,26,2048]{3,0,2,1:T(4,128)}), f32[4,8,26,2048]{3,0,2,1:T(4,128)}, u32[]{:S(2)}, u32[]{:S(2)}) async-start(f32[4,8,26,2048]{3,0,2,1:T(4,128)} %copy.63), calls=%async_computation.5 | async-start | bytes 13631488 | tf_op jit(solution)/shard_map/all_to_all | solution.py:92
  477.3 5.5 copy-start.3
  477.3 5.5 copy-start.7
  482.8 3.5 copy-start.4
  482.8 3.5 copy-start.13
  482.8 3.5 copy-start.14
  596.9 10.5 %copy-start.1 = (bf16[1,2048,384]{2,1,0:T(8,128)(2,1)S(1)}, bf16[1,2048,384]{2,1,0:T(8,128)(2,1)}, u32[]{:S(2)}) copy-start(bf16[1,2048,384]{2,1,0:T(8,128)(2,1)} %param.11) | copy-start | bytes 4718596
where the time goes:
time: 618 us; the launch traced here: 608 us
  waiting for transfers between devices  245 us (40%)
  blocking collectives  149 us (24%)
  local copies, waits for them, and re-layouts  135 us (22%)
  matrix products  35.5 us (6%)
  starting transfers between devices  25.9 us (4%)
  other arithmetic  15.7 us (3%)
    all_to_all x1, blocking collectives, per_device(): lax.all_to_all(partial_grid, 'rep', split_axis=0, concat_axis=0, tiled=True)  149 us
    all_to_all x1, waiting for transfers between devices, per_device(): lax.all_to_all(send_grad, 'rep', split_axis=0, concat_axis=0, tiled=True)  69.5 us
    all_to_all x1, waiting for transfers between devices, per_device(): lax.all_to_all(lax.all_to_all(partial_grid, 'rep', split_axis=0, concat_a...  64.7 us
    all_to_all x1, waiting for transfers between devices, per_device(): lax.all_to_all(send_in, 'rep', split_axis=0, concat_axis=0, tiled=True)  55 us
    all_to_all x1, waiting for transfers between devices, per_device(): lax.all_to_all(lax.all_to_all(send_in, 'rep', split_axis=0, concat_axis=0...  34.3 us
    all_to_all x1, waiting for transfers between devices, per_device(): lax.all_to_all(lax.all_to_all(send_grad, 'rep', split_axis=0, concat_axis...  21.8 us
    reshape x2, local copies, waits for them, and re-layouts, per_device(): partial_rows.reshape(rep_count, exp_count, capacity, features)  14.2 us
    another operation x2, local copies, waits for them, and re-layouts, per_device(): jnp.repeat(packed_grad.reshape(experts, capacity, features), 2, axis=0)  12.4 us
  transfers between devices with their start and end apart: 5, of which 5 were waited for; matrix products, arithmetic and copies ran while one was open for 11% of the time, Pallas kernels for 0%

commit v1 on v0

--- a/solution.py
+++ b/solution.py
@@ -1,10 +1,159 @@
+import functools
+
 import jax
 import jax.numpy as jnp
 from jax import lax
+from jax.experimental import pallas as pl
+from jax.experimental.pallas import tpu as pltpu
 from jax.sharding import PartitionSpec as P
 
 
-def per_device(tokens, grad_out, expert_ids, gate_probs, gate_weight, up_weight, down_weight):
+AXES = ("rep", "exp")
+
+
+def flip_pairs(move):
+    pairs = []
+    for z in range(4):
+        for y in range(2):
+            for x in range(2):
+                for c in range(2):
+                    tz, ty, tx, tc = move(z, y, x, c)
+                    pairs.append((((z * 2 + y) * 2 + x) * 2 + c, ((tz * 2 + ty) * 2 + tx) * 2 + tc))
+    return pairs
+
+
+OTHER_CORE = flip_pairs(lambda z, y, x, c: (z, y, x, 1 - c))
+FIRST_FLIP = flip_pairs(lambda z, y, x, c: (z, y, 1 - x, c) if c == 0 else (z, 1 - y, x, c))
+SECOND_FLIP = flip_pairs(lambda z, y, x, c: (z, 1 - y, x, c) if c == 0 else (z, y, 1 - x, c))
+SHIFTS = (0, 3, 2, 1)
+Z_IN = [flip_pairs(lambda z, y, x, c, s=s: ((z - s) % 4, y, x, c)) for s in SHIFTS]
+Z_BACK = [flip_pairs(lambda z, y, x, c, s=s: ((z + s) % 4, y, x, c)) for s in SHIFTS]
+LAST = (((1,), (1,)), ((), ()))
+FIRST = (((0,), (0,)), ((), ()))
+F32, B16 = jnp.float32, jnp.bfloat16
+
+
+def move(value, pairs):
+    return lax.ppermute(value, AXES, pairs)
+
+
+def chunk_kernel(features, half, rows, *refs):
+    wanted, blocks, in_mat, down_mat = refs[0], refs[1:5], refs[5], refs[6]
+    rows_out, scaled_out, gate_out, up_out, hidden_out, keep, send = refs[-8:-1]
+    total = refs[-1]
+    step = pl.program_id(0)
+
+    @pl.when(step == 0)
+    def _():
+        for i, block in enumerate(blocks):
+            place = pl.ds(i * rows, rows)
+            rows_out[place, :] = block[:, :features]
+            terms = jnp.where(wanted[...] > 0.0, block[:, 2 * features :].astype(F32), 0.0)
+            weight = jnp.sum(terms, axis=1, keepdims=True)
+            scaled_out[place, :] = (weight * block[:, features : 2 * features].astype(F32)).astype(B16)
+
+    pre = jnp.dot(rows_out[...], in_mat[0], preferred_element_type=F32)
+    gate_pre, up_pre = pre[:, :half], pre[:, half:]
+    hidden_grad = lax.dot_general(scaled_out[...], down_mat[0], LAST, preferred_element_type=F32)
+    sigmoid_gate = jax.nn.sigmoid(gate_pre)
+    activated = gate_pre * sigmoid_gate
+    hidden_out[0] = (activated * up_pre).astype(B16)
+    up_in = (hidden_grad * activated).astype(B16)
+    gate_in = (hidden_grad * up_pre * sigmoid_gate * (1.0 + gate_pre * (1.0 - sigmoid_gate))).astype(B16)
+    gate_out[0] = gate_in
+    up_out[0] = up_in
+    part = lax.dot_general(jnp.concatenate([gate_in, up_in], axis=1), in_mat[0], LAST, preferred_element_type=F32)
+
+    @pl.when(step == 0)
+    def _():
+        total[...] = part
+
+    @pl.when(step == 1)
+    def _():
+        keep[...] = total[: 2 * rows, :] + part[: 2 * rows]
+        send[...] = (total[2 * rows :, :] + part[2 * rows :]).astype(B16)
+
+
+def chunk_call(place, chunks, wanted, blocks, in_mats, down_mats, stacks):
+    rows, width = blocks[0].shape
+    features = down_mats.shape[2]
+    half = down_mats.shape[1]
+    many = 4 * rows
+    whole = lambda shape: pl.BlockSpec(shape, lambda j: (0,) * len(shape))
+    wide = pl.BlockSpec((many, features), lambda j: (place, 0))
+    thin = pl.BlockSpec((1, many, half), lambda j: (j, place, 0))
+    in_specs = [whole(wanted.shape)] + [whole((rows, width))] * 4 + [
+        pl.BlockSpec((1,) + in_mats.shape[1:], lambda j: (j, 0, 0)),
+        pl.BlockSpec((1,) + down_mats.shape[1:], lambda j: (j, 0, 0)),
+    ]
+    operands = [wanted, *blocks, in_mats, down_mats]
+    aliases = {}
+    if stacks is not None:
+        aliases = {len(operands) + i: i for i in range(5)}
+        in_specs += [pl.BlockSpec(memory_space=pl.ANY)] * 5
+        operands += list(stacks)
+    return pl.pallas_call(
+        functools.partial(chunk_kernel, features, half, rows),
+        grid=(2,),
+        out_shape=[jax.ShapeDtypeStruct((chunks * many, features), B16)] * 2
+        + [jax.ShapeDtypeStruct((2, chunks * many, half), B16)] * 3
+        + [jax.ShapeDtypeStruct((2 * rows, features), F32), jax.ShapeDtypeStruct((2 * rows, features), B16)],
+        in_specs=in_specs,
+        out_specs=[wide, wide, thin, thin, thin, whole((2 * rows, features)), whole((2 * rows, features))],
+        scratch_shapes=[pltpu.VMEM((many, features), F32)],
+        input_output_aliases=aliases,
+        cost_estimate=pl.CostEstimate(
+            flops=2 * 10 * many * features * half, bytes_accessed=24 * 1024 * 1024, transcendentals=2 * many * half
+        ),
+        compiler_params=pltpu.CompilerParams(vmem_limit_bytes=40 * 1024 * 1024),
+    )(*operands)
+
+
+def dense_device(tokens, grad_out, expert_ids, gate_probs, gate_weight, up_weight, down_weight):
+    rows, _ = tokens.shape
+    experts = lax.axis_size("rep") * lax.axis_size("exp") // 2
+    mine = (lax.axis_index("rep") * lax.axis_size("exp") + lax.axis_index("exp")) // 2
+
+    in_own = jnp.concatenate([gate_weight[0], up_weight[0]], axis=1)
+    in_mats = jnp.stack([in_own, move(in_own, OTHER_CORE)])
+    down_mats = jnp.stack([down_weight[0], move(down_weight[0], OTHER_CORE)])
+
+    chosen = expert_ids[:, :, None] == jnp.arange(experts, dtype=jnp.int32)
+    dense = jnp.sum(jnp.where(chosen, gate_probs[:, :, None], 0.0), axis=1)
+    high = lax.reduce_precision(dense, 8, 7)
+    middle = lax.reduce_precision(dense - high, 8, 7)
+    low = dense - high - middle
+    terms = jnp.concatenate([high, middle, low], axis=1).astype(B16)
+    pad = -terms.shape[1] % 128
+    block = jnp.concatenate([tokens, grad_out, jnp.pad(terms, ((0, 0), (0, pad)))], axis=1)
+    lanes = jnp.arange(3 * experts + pad, dtype=jnp.int32)
+    wanted = ((lanes < 3 * experts) & (lanes % experts == mine)).astype(F32)[None]
+
+    stacks, totals = None, []
+    for step in range(4):
+        own = block if step == 0 else move(block, Z_IN[step])
+        first = move(own, FIRST_FLIP)
+        blocks = [own, first, move(own, SECOND_FLIP), move(first, SECOND_FLIP)]
+        *stacks, keep, send = chunk_call(step, 4, wanted, blocks, in_mats, down_mats, stacks)
+        partial = keep + move(send, SECOND_FLIP).astype(F32)
+        partial = partial[:rows] + move(partial[rows:].astype(B16), FIRST_FLIP).astype(F32)
+        if step > 0:
+            partial = move(partial.astype(B16), Z_BACK[step]).astype(F32)
+        totals.append(partial)
+    token_grad = (totals[0] + totals[1] + totals[2] + totals[3]).astype(B16)
+    all_in, all_scaled, all_gate, all_up, all_hidden = stacks
+
+    def grads(part):
+        pairs = ((all_in, all_gate[part]), (all_in, all_up[part]), (all_hidden[part], all_scaled))
+        return [lax.dot_general(a, b, FIRST, preferred_element_type=F32) for a, b in pairs]
+
+    other = [value.astype(B16) for value in grads(1)]
+    arrived = [move(value, OTHER_CORE) for value in other]
+    summed = [(here + there.astype(F32)).astype(B16)[None] for here, there in zip(grads(0), arrived)]
+    return (token_grad, *summed)
+
+
+def sparse_device(tokens, grad_out, expert_ids, gate_probs, gate_weight, up_weight, down_weight):
     rep_count = lax.axis_size("rep")
     exp_count = lax.axis_size("exp")
     tok_rows, features = tokens.shape
@@ -106,6 +255,13 @@
     return (token_grad, gate_grad, up_grad, down_grad)
 
 
+def per_device(tokens, grad_out, expert_ids, *rest):
+    experts = lax.axis_size("rep") * lax.axis_size("exp") // 2
+    if lax.axis_size("rep") == 4 and lax.axis_size("exp") == 8 and 2 * expert_ids.shape[1] >= experts:
+        return dense_device(tokens, grad_out, expert_ids, *rest)
+    return sparse_device(tokens, grad_out, expert_ids, *rest)
+
+
 def solution(mesh):
     return jax.shard_map(
         per_device,

time: 618 us -> 155 us (0.25); the launches traced: 608 us -> 155 us
  waiting for transfers between devices: 245 us -> 46.9 us
  blocking collectives: 149 us -> 0 us
  local copies, waits for them, and re-layouts: 135 us -> 0.27 us
  Pallas kernels: 0 us -> 32.3 us
  matrix products: 35.5 us -> 13.9 us
  starting transfers between devices: 25.9 us -> 45.4 us
    all_to_all x5 -> x0, waiting for transfers between devices: 245 us -> none  [the longest x1 69.5 us: per_device(): lax.all_to_all(send_grad, 'rep', split_axis=0, concat_axis=0, tiled=True)]
    all_to_all x1 -> x0, blocking collectives: 149 us -> none  [per_device(): lax.all_to_all(partial_grid, 'rep', split_axis=0, concat_axis=0, tiled=True)]
    ppermute x0 -> x31, waiting for transfers between devices: none -> 46.9 us  [move(): return lax.ppermute(value, AXES, pairs)]
    ppermute x0 -> x31, starting transfers between devices: none -> 45.4 us  [move(): return lax.ppermute(value, AXES, pairs)]
    reshape x11 -> x0, local copies, waits for them, and re-layouts: 45 us -> none  [the longest x2 14.2 us: per_device(): partial_rows.reshape(rep_count, exp_count, capacity, features)]
    all_to_all x6 -> x0, local copies, waits for them, and re-layouts: 43.8 us -> none  [the longest x1 12.1 us: per_device(): lax.all_to_all(lax.all_to_all(partial_grid, 'rep', split_axis=0, concat_a...]
    pallas_call x0 -> x4, Pallas kernels: none -> 32.3 us  [chunk_call(): pl.pallas_call(functools.partial(chunk_kernel, features, half, rows), gri...]
    all_to_all x5 -> x0, starting transfers between devices: 25.9 us -> none  [the longest x1 6.48 us: per_device(): lax.all_to_all(send_in, 'rep', split_axis=0, concat_axis=0, tiled=True)]
  transfers between devices with their start and end apart: 5 -> 31, of which waited for: 5 -> 8; matrix products, arithmetic and copies ran while one was open for 11% -> 13% of each run, Pallas kernels for 0% -> 16%
where the time goes in v1:
time: 155 us
  waiting for transfers between devices  46.9 us (30%)
  starting transfers between devices  45.4 us (29%)
  Pallas kernels  32.3 us (21%)
  other arithmetic  15.4 us (10%)
  matrix products  13.9 us (9%)
    ppermute x31, waiting for transfers between devices, move(): return lax.ppermute(value, AXES, pairs)  46.9 us
    ppermute x31, starting transfers between devices, move(): return lax.ppermute(value, AXES, pairs)  45.4 us
    pallas_call x4, Pallas kernels, chunk_call(): pl.pallas_call(functools.partial(chunk_kernel, features, half, rows), gri...  32.3 us
    dot_general x6, matrix products, grads(): lax.dot_general(a, b, FIRST, preferred_element_type=F32)  13.9 us
    another operation x2, other arithmetic, dense_device(): in_mats = jnp.stack([in_own, move(in_own, OTHER_CORE)])  10 us
    another operation x1, other arithmetic, dense_device(): down_mats = jnp.stack([down_weight[0], move(down_weight[0], OTHER_CORE)])  4.01 us
  transfers between devices with their start and end apart: 31, of which 8 were waited for; matrix products, arithmetic and copies ran while one was open for 13% of the time, Pallas kernels for 16%

profile of v1, /device:TPU:0, one launch (start us, length us, event | category | flops | bytes accessed | tf_op | source)
XLA Modules:
  0.0 155.1 jit_solution(8683709136939118941)
XLA Ops:
  0.7 4.9 %fusion.28 = (bf16[1,2048,768]{2,1,0:T(8,128)(2,1)}, bf16[2048,768]{1,0:T(8,128)(2,1)}) fusion(bf16[2048,384]{1,0:T(8,128)(2,1)} %bitcast.37, bf16[2048,384]{1,0:T(8,128)(2,1)} %bitcast.38), kind=kLoop, calls=%fused_computation.57 | loop fusion | flops 6291456 | bytes 9437184 | tf_op jit(solution)/shard_map/stack | solution.py:118
  5.6 0.5 collective-permute-start.3
  6.1 0.0 collective-permute-start.4
  6.1 0.1 copy.31
  6.2 0.1 copy.30
  6.3 0.1 fusion.27
  6.4 3.0 %collective-permute-start = (bf16[48,4224]{1,0:T(8,128)(2,1)S(1)}, bf16[48,4224]{1,0:T(8,128)(2,1)S(1)}, u32[]{:S(2)}, u32[]{:S(2)}) collective-permute-start(bf16[48,4224]{1,0:T(8,128)(2,1)S(1)} %pad_maximum_fusion.3.refs_1_), channel_id=1, source_target_pairs={{0,2},{1,5},{2,0},{3,7},{4,6},{5,1},{6,4},{7,3},{8,10},{9,13},{10,... | collective-permute-start | bytes 1216520 | tf_op jit(solution)/shard_map/ppermute | solution.py:37
  9.5 1.5 collective-permute-start.1
  11.0 1.6 %collective-permute-start.7 = (bf16[48,4224]{1,0:T(8,128)(2,1)S(1)}, bf16[48,4224]{1,0:T(8,128)(2,1)S(1)}, u32[]{:S(2)}, u32[]{:S(2)}) collective-permute-start(bf16[48,4224]{1,0:T(8,128)(2,1)S(1)} %pad_maximum_fusion.3.refs_1_), channel_id=1, source_target_pairs={{0,8},{1,9},{2,10},{3,11},{4,12},{5,13},{6,14},{7,15},{8,16},{9,17... | collective-permute-start | bytes 1216520 | tf_op jit(solution)/shard_map/ppermute | solution.py:37
  12.6 6.4 %collective-permute-done.refs_2_ = bf16[48,4224]{1,0:T(8,128)(2,1)S(1)} collective-permute-done((bf16[48,4224]{1,0:T(8,128)(2,1)S(1)}, bf16[48,4224]{1,0:T(8,128)(2,1)S(1)}, u32[]{:S(2)}, u32[]{:S(2)}) %collective-permute-start) | collective-permute-done | bytes 405536 | tf_op jit(solution)/shard_map/ppermute | solution.py:37
  19.0 3.6 %collective-permute-start.14 = (bf16[48,4224]{1,0:T(8,128)(2,1)S(1)}, bf16[48,4224]{1,0:T(8,128)(2,1)S(1)}, u32[]{:S(2)}, u32[]{:S(2)}) collective-permute-start(bf16[48,4224]{1,0:T(8,128)(2,1)S(1)} %pad_maximum_fusion.3.refs_1_), channel_id=1, source_target_pairs={{0,16},{1,17},{2,18},{3,19},{4,20},{5,21},{6,22},{7,23},{8,24},{9,... | collective-permute-start | bytes 1216520 | tf_op jit(solution)/shard_map/ppermute | solution.py:37
  22.5 0.0 collective-permute-done.1.refs_3_
  22.5 1.3 collective-permute-start.21
  23.9 1.3 collective-permute-done.7.refs_1_
  25.1 0.2 collective-permute-start.8
  25.4 15.7 %collective-permute-done.14.refs_1_ = bf16[48,4224]{1,0:T(8,128)(2,1)S(1)} collective-permute-done((bf16[48,4224]{1,0:T(8,128)(2,1)S(1)}, bf16[48,4224]{1,0:T(8,128)(2,1)S(1)}, u32[]{:S(2)}, u32[]{:S(2)}) %collective-permute-start.14) | collective-permute-done | bytes 405536 | tf_op jit(solution)/shard_map/ppermute | solution.py:37
  41.1 0.5 collective-permute-start.2
  41.6 0.0 collective-permute-done.4
  41.6 1.3 collective-permute-start.15
  42.9 4.0 %pad_maximum_fusion.2.refs_6_ = bf16[2,384,2048]{2,1,0:T(8,128)(2,1)} fusion(bf16[1,384,2048]{2,1,0:T(8,128)(2,1)} %bitcast.5, bf16[1,384,2048]{2,1,0:T(8,128)(2,1)} %param.13), kind=kLoop, calls=%fused_computation.2 | loop fusion | flops 1572864 | bytes 6291456 | tf_op jit(solution)/shard_map/stack | solution.py:119
  46.9 0.7 collective-permute-start.9
  47.7 1.5 collective-permute-start.22
  49.2 0.5 collective-permute-start.10
  49.7 5.1 %pad_maximum_fusion.refs_5_ = bf16[2,2048,768]{2,1,0:T(8,128)(2,1)} fusion(bf16[1,2048,768]{2,1,0:T(8,128)(2,1)} %bitcast.3, bf16[1,2048,768]{2,1,0:T(8,128)(2,1)S(1)} %copy-done), kind=kLoop, calls=%fused_computation | loop fusion | flops 3145728 | bytes 12582912 | tf_op jit(solution)/shard_map/stack | solution.py:118
  54.8 1.5 collective-permute-start.16
  56.3 0.5 collective-permute-start.17
  56.8 8.0 %shard_map.102 = (bf16[768,2048]{1,0:T(8,128)(2,1)S(1)}, bf16[768,2048]{1,0:T(8,128)(2,1)S(1)}, bf16[2,768,384]{2,1,0:T(8,128)(2,1)S(1)}, bf16[2,768,384]{2,1,0:...) custom-call(f32[1,128]{1,0:T(1,128)S(1)} %and_convert_fusion.refs_0_, ...), custom_call_target="tpu_custom_call" | custom-call | flops 3019898880 | bytes 25165824 | tf_op jit(solution)/shard_map/pallas_call | solution.py:95
  64.9 1.6 %collective-permute-start.23 = (bf16[48,4224]{1,0:T(8,128)(2,1)S(1)}, bf16[48,4224]{1,0:T(8,128)(2,1)S(1)}, u32[]{:S(2)}, u32[]{:S(2)}) collective-permute-start(bf16[48,4224]{1,0:T(8,128)(2,1)S(1)} %collective-permute-done.21.refs_1_), channel_id=1, source_target_pairs={{0,4},{1,3},{2,6},{3,1},{4,0},{5,7},{6,2},{7,5},{8,12},{9,11},{10,... | collective-permute-start | bytes 1216520 | tf_op jit(solution)/shard_map/ppermute | solution.py:37
  66.4 0.5 collective-permute-start.24
  67.0 8.0 %shard_map.103 = (bf16[768,2048]{1,0:T(8,128)(2,1)S(1)}, bf16[768,2048]{1,0:T(8,128)(2,1)S(1)}, bf16[2,768,384]{2,1,0:T(8,128)(2,1)S(1)}, bf16[2,768,384]{2,1,0:...) custom-call(f32[1,128]{1,0:T(1,128)S(1)} %and_convert_fusion.refs_0_, ...), custom_call_target="tpu_custom_call", output_to_operand_aliasing={{0}: (7, {}), {1}: (8, {}), {2}: (9, {}), {3}: (10, {}), {4... | custom-call | flops 3019898880 | bytes 25165824 | tf_op jit(solution)/shard_map/pallas_call | solution.py:95
  75.0 8.0 %shard_map.104 = (bf16[768,2048]{1,0:T(8,128)(2,1)S(1)}, bf16[768,2048]{1,0:T(8,128)(2,1)S(1)}, bf16[2,768,384]{2,1,0:T(8,128)(2,1)S(1)}, bf16[2,768,384]{2,1,0:...) custom-call(f32[1,128]{1,0:T(1,128)S(1)} %and_convert_fusion.refs_0_, ...), custom_call_target="tpu_custom_call", output_to_operand_aliasing={{0}: (7, {}), {1}: (8, {}), {2}: (9, {}), {3}: (10, {}), {4... | custom-call | flops 3019898880 | bytes 25165824 | tf_op jit(solution)/shard_map/pallas_call | solution.py:95
  83.1 8.2 %shard_map.105 = (bf16[768,2048]{1,0:T(8,128)(2,1)S(1)}, bf16[768,2048]{1,0:T(8,128)(2,1)S(1)}, bf16[2,768,384]{2,1,0:T(8,128)(2,1)S(1)}, bf16[2,768,384]{2,1,0:...) custom-call(f32[1,128]{1,0:T(1,128)S(1)} %and_convert_fusion.refs_0_, ...), custom_call_target="tpu_custom_call", output_to_operand_aliasing={{0}: (7, {}), {1}: (8, {}), {2}: (9, {}), {3}: (10, {}), {4... | custom-call | flops 3019898880 | bytes 25165824 | tf_op jit(solution)/shard_map/pallas_call | solution.py:95
  91.3 1.4 convolution_convert_fusion
  92.7 0.1 collective-permute-start.30
  92.8 1.6 %collective-permute-start.11 = (bf16[96,2048]{1,0:T(8,128)(2,1)S(1)}, bf16[96,2048]{1,0:T(8,128)(2,1)S(1)}, u32[]{:S(2)}, u32[]{:S(2)}) collective-permute-start(bf16[96,2048]{1,0:T(8,128)(2,1)S(1)} %get-tuple-element.40), channel_id=1, source_target_pairs={{0,4},{1,3},{2,6},{3,1},{4,0},{5,7},{6,2},{7,5},{8,12},{9,11},{10,... | collective-permute-start | bytes 1179656 | tf_op jit(solution)/shard_map/ppermute | solution.py:37
  94.4 1.9 %convolution_convert_fusion.1 = bf16[2048,384]{1,0:T(8,128)(2,1)S(1)} fusion(bf16[768,2048]{1,0:T(8,128)(2,1)S(1)} %get-tuple-element.55, bf16[2,768,384]{2,1,0:T(8,128)(2,1)S(1)} %get-tuple-element.57), kind=kOutput, calls=%fused_computation.7 | convolution fusion | flops 1208745984 | bytes 5308416 | tf_op jit(solution)/shard_map/dot_general | solution.py:148
  96.3 0.1 collective-permute-start.29
  96.3 0.7 collective-permute-start.18
  97.0 1.4 collective-permute-start.25
  98.4 2.2 %collective-permute-done.11 = bf16[96,2048]{1,0:T(8,128)(2,1)S(1)} collective-permute-done((bf16[96,2048]{1,0:T(8,128)(2,1)S(1)}, bf16[96,2048]{1,0:T(8,128)(2,1)S(1)}, u32[]{:S(2)}, u32[]{:S(2)}) %collective-permute-start.11) | collective-permute-done | bytes 393248 | tf_op jit(solution)/shard_map/ppermute | solution.py:37
  100.6 1.5 collective-permute-start.5
  102.2 0.1 convert_add_fusion.2
  102.3 2.6 %collective-permute-done.18 = bf16[96,2048]{1,0:T(8,128)(2,1)S(1)} collective-permute-done((bf16[96,2048]{1,0:T(8,128)(2,1)S(1)}, bf16[96,2048]{1,0:T(8,128)(2,1)S(1)}, u32[]{:S(2)}, u32[]{:S(2)}) %collective-permute-start.18) | collective-permute-done | bytes 393248 | tf_op jit(solution)/shard_map/ppermute | solution.py:37
  104.8 1.3 collective-permute-start.12
  106.2 0.1 convert_add_fusion.1
  106.3 4.8 %collective-permute-done.25 = bf16[96,2048]{1,0:T(8,128)(2,1)S(1)} collective-permute-done((bf16[96,2048]{1,0:T(8,128)(2,1)S(1)}, bf16[96,2048]{1,0:T(8,128)(2,1)S(1)}, u32[]{:S(2)}, u32[]{:S(2)}) %collective-permute-start.25) | collective-permute-done | bytes 393248 | tf_op jit(solution)/shard_map/ppermute | solution.py:37
  111.1 1.3 collective-permute-start.19
  112.4 0.1 convert_add_fusion
  112.5 4.9 %collective-permute-done.5 = bf16[96,2048]{1,0:T(8,128)(2,1)S(1)} collective-permute-done((bf16[96,2048]{1,0:T(8,128)(2,1)S(1)}, bf16[96,2048]{1,0:T(8,128)(2,1)S(1)}, u32[]{:S(2)}, u32[]{:S(2)}) %collective-permute-start.5) | collective-permute-done | bytes 393248 | tf_op jit(solution)/shard_map/ppermute | solution.py:37
  117.5 1.3 collective-permute-start.26
  118.8 0.1 convert_add_fusion.3
  118.9 0.8 collective-permute-start.6
  119.8 10.8 %collective-permute-start.13 = (bf16[48,2048]{1,0:T(8,128)(2,1)S(1)}, bf16[48,2048]{1,0:T(8,128)(2,1)S(1)}, u32[]{:S(2)}, u32[]{:S(2)}) collective-permute-start(bf16[48,2048]{1,0:T(8,128)(2,1)S(1)} %fusion.17), channel_id=1, source_target_pairs={{0,24},{1,25},{2,26},{3,27},{4,28},{5,29},{6,30},{7,31},{8,0},{9,1... | collective-permute-start | bytes 589832 | tf_op jit(solution)/shard_map/ppermute | solution.py:37
  130.6 0.1 fusion.16
  130.7 0.1 collective-permute-start.20
  130.8 0.1 fusion.15
  130.8 3.8 %collective-permute-start.27 = (bf16[48,2048]{1,0:T(8,128)(2,1)S(1)}, bf16[48,2048]{1,0:T(8,128)(2,1)S(1)}, u32[]{:S(2)}, u32[]{:S(2)}) collective-permute-start(bf16[48,2048]{1,0:T(8,128)(2,1)S(1)} %fusion.15), channel_id=1, source_target_pairs={{0,8},{1,9},{2,10},{3,11},{4,12},{5,13},{6,14},{7,15},{8,16},{9,17... | collective-permute-start | bytes 589832 | tf_op jit(solution)/shard_map/ppermute | solution.py:37
  134.6 1.9 %convolution_convert_fusion.2 = bf16[2048,384]{1,0:T(8,128)(2,1)S(1)} fusion(bf16[768,2048]{1,0:T(8,128)(2,1)S(1)} %get-tuple-element.55, bf16[2,768,384]{2,1,0:T(8,128)(2,1)S(1)} %get-tuple-element.56), kind=kOutput, calls=%fused_computation.8 | convolution fusion | flops 1208745984 | bytes 5308416 | tf_op jit(solution)/shard_map/dot_general | solution.py:148
  136.5 0.1 collective-permute-start.28
  136.6 8.9 %collective-permute-done.20 = bf16[48,2048]{1,0:T(8,128)(2,1)S(1)} collective-permute-done((bf16[48,2048]{1,0:T(8,128)(2,1)S(1)}, bf16[48,2048]{1,0:T(8,128)(2,1)S(1)}, u32[]{:S(2)}, u32[]{:S(2)}) %collective-permute-start.20) | collective-permute-done | bytes 196640 | tf_op jit(solution)/shard_map/ppermute | solution.py:37
  145.5 0.8 fusion.21
  146.3 2.6 %fusion.2 = bf16[1,384,2048]{2,1,0:T(8,128)(2,1)} fusion(bf16[384,2048]{1,0:T(8,128)(2,1)S(1)} %collective-permute-done.30, bf16[768,2048]{1,0:T(8,128)(2,1)S(1)} %get-tuple-element.59, bf16[2,768,384]{2,1,0:T(8,128)(2,1)S(1)} %get-tuple-element.58), kind=kOutput, calls=%fused_computation.11 | convolution fusion | flops 1210318848 | bytes 6881280 | tf_op jit(solution)/shard_map/dot_general | solution.py:148
  149.0 3.1 %fusion.1 = bf16[1,2048,384]{2,1,0:T(8,128)(2,1)} fusion(bf16[2048,384]{1,0:T(8,128)(2,1)S(1)} %collective-permute-done.29, bf16[768,2048]{1,0:T(8,128)(2,1)S(1)} %get-tuple-element.55, bf16[2,768,384]{2,1,0:T(8,128)(2,1)S(1)} %get-tuple-element.57), kind=kOutput, calls=%fused_computation.10 | convolution fusion | flops 1210318848 | bytes 6881280 | tf_op jit(solution)/shard_map/dot_general | solution.py:148
  152.0 3.0 %fusion = bf16[1,2048,384]{2,1,0:T(8,128)(2,1)} fusion(bf16[2048,384]{1,0:T(8,128)(2,1)S(1)} %collective-permute-done.28, bf16[768,2048]{1,0:T(8,128)(2,1)S(1)} %get-tuple-element.55, bf16[2,768,384]{2,1,0:T(8,128)(2,1)S(1)} %get-tuple-element.56), kind=kOutput, calls=%fused_computation.9 | convolution fusion | flops 1210318848 | bytes 6881280 | tf_op jit(solution)/shard_map/dot_general | solution.py:148
  (41 shorter events, 0.3 us)
Async XLA Ops:
  0.6 5.5 %copy-start.3 = (f32[48,8]{0,1:T(8,128)S(1)}, f32[48,8]{0,1:T(8,128)}, u32[]{:S(2)}) copy-start(f32[48,8]{0,1:T(8,128)} %param.10) | copy-start | bytes 4612
  0.6 5.5 %copy-start.4 = (s32[48,8]{0,1:T(8,128)S(1)}, s32[48,8]{0,1:T(8,128)}, u32[]{:S(2)}) copy-start(s32[48,8]{0,1:T(8,128)} %param.9) | copy-start | bytes 4612
  0.7 5.7 %copy-start.1 = (bf16[48,2048]{1,0:T(8,128)(2,1)S(1)}, bf16[48,2048]{1,0:T(8,128)(2,1)}, u32[]{:S(2)}) copy-start(bf16[48,2048]{1,0:T(8,128)(2,1)} %param.8) | copy-start | bytes 589828
  0.7 5.7 %copy-start.2 = (bf16[48,2048]{1,0:T(8,128)(2,1)S(1)}, bf16[48,2048]{1,0:T(8,128)(2,1)}, u32[]{:S(2)}) copy-start(bf16[48,2048]{1,0:T(8,128)(2,1)} %param.7) | copy-start | bytes 589828
  5.6 43.6 %collective-permute-start.3 = (bf16[2048,768]{1,0:T(8,128)(2,1)}, bf16[2048,768]{1,0:T(8,128)(2,1)}, u32[]{:S(2)}, u32[]{:S(2)}) collective-permute-start(bf16[2048,768]{1,0:T(8,128)(2,1)} %get-tuple-element.61), channel_id=1, source_target_pairs={{0,1},{1,0},{2,3},{3,2},{4,5},{5,4},{6,7},{7,6},{8,9},{9,8},{10,11... | collective-permute-start | bytes 9437192 | tf_op jit(solution)/shard_map/ppermute | solution.py:37
  6.1 35.5 %collective-permute-start.4 = (bf16[384,2048]{1,0:T(8,128)(2,1)}, bf16[384,2048]{1,0:T(8,128)(2,1)}, u32[]{:S(2)}, u32[]{:S(2)}) collective-permute-start(bf16[384,2048]{1,0:T(8,128)(2,1)} %bitcast.4), channel_id=1, source_target_pairs={{0,1},{1,0},{2,3},{3,2},{4,5},{5,4},{6,7},{7,6},{8,9},{9,8},{10,11... | collective-permute-start | bytes 4718600 | tf_op jit(solution)/shard_map/ppermute | solution.py:37
  6.4 12.5 %collective-permute-start = (bf16[48,4224]{1,0:T(8,128)(2,1)S(1)}, bf16[48,4224]{1,0:T(8,128)(2,1)S(1)}, u32[]{:S(2)}, u32[]{:S(2)}) collective-permute-start(bf16[48,4224]{1,0:T(8,128)(2,1)S(1)} %pad_maximum_fusion.3.refs_1_), channel_id=1, source_target_pairs={{0,2},{1,5},{2,0},{3,7},{4,6},{5,1},{6,4},{7,3},{8,10},{9,13},{10,... | collective-permute-start | bytes 1216520 | tf_op jit(solution)/shard_map/ppermute | solution.py:37
  9.5 13.1 %collective-permute-start.1 = (bf16[48,4224]{1,0:T(8,128)(2,1)S(1)}, bf16[48,4224]{1,0:T(8,128)(2,1)S(1)}, u32[]{:S(2)}, u32[]{:S(2)}) collective-permute-start(bf16[48,4224]{1,0:T(8,128)(2,1)S(1)} %pad_maximum_fusion.3.refs_1_), channel_id=1, source_target_pairs={{0,4},{1,3},{2,6},{3,1},{4,0},{5,7},{6,2},{7,5},{8,12},{9,11},{10,... | collective-permute-start | bytes 1216520 | tf_op jit(solution)/shard_map/ppermute | solution.py:37
  11.0 14.2 %collective-permute-start.7 = (bf16[48,4224]{1,0:T(8,128)(2,1)S(1)}, bf16[48,4224]{1,0:T(8,128)(2,1)S(1)}, u32[]{:S(2)}, u32[]{:S(2)}) collective-permute-start(bf16[48,4224]{1,0:T(8,128)(2,1)S(1)} %pad_maximum_fusion.3.refs_1_), channel_id=1, source_target_pairs={{0,8},{1,9},{2,10},{3,11},{4,12},{5,13},{6,14},{7,15},{8,16},{9,17... | collective-permute-start | bytes 1216520 | tf_op jit(solution)/shard_map/ppermute | solution.py:37
  19.0 22.1 %collective-permute-start.14 = (bf16[48,4224]{1,0:T(8,128)(2,1)S(1)}, bf16[48,4224]{1,0:T(8,128)(2,1)S(1)}, u32[]{:S(2)}, u32[]{:S(2)}) collective-permute-start(bf16[48,4224]{1,0:T(8,128)(2,1)S(1)} %pad_maximum_fusion.3.refs_1_), channel_id=1, source_target_pairs={{0,16},{1,17},{2,18},{3,19},{4,20},{5,21},{6,22},{7,23},{8,24},{9,... | collective-permute-start | bytes 1216520 | tf_op jit(solution)/shard_map/ppermute | solution.py:37
  22.5 24.4 %collective-permute-start.21 = (bf16[48,4224]{1,0:T(8,128)(2,1)S(1)}, bf16[48,4224]{1,0:T(8,128)(2,1)S(1)}, u32[]{:S(2)}, u32[]{:S(2)}) collective-permute-start(bf16[48,4224]{1,0:T(8,128)(2,1)S(1)} %pad_maximum_fusion.3.refs_1_), channel_id=1, source_target_pairs={{0,24},{1,25},{2,26},{3,27},{4,28},{5,29},{6,30},{7,31},{8,0},{9,1... | collective-permute-start | bytes 1216520 | tf_op jit(solution)/shard_map/ppermute | solution.py:37
  25.1 22.5 %collective-permute-start.8 = (bf16[48,4224]{1,0:T(8,128)(2,1)S(1)}, bf16[48,4224]{1,0:T(8,128)(2,1)S(1)}, u32[]{:S(2)}, u32[]{:S(2)}) collective-permute-start(bf16[48,4224]{1,0:T(8,128)(2,1)S(1)} %collective-permute-done.7.refs_1_), channel_id=1, source_target_pairs={{0,2},{1,5},{2,0},{3,7},{4,6},{5,1},{6,4},{7,3},{8,10},{9,13},{10,... | collective-permute-start | bytes 1216520 | tf_op jit(solution)/shard_map/ppermute | solution.py:37
  41.1 13.7 %collective-permute-start.2 = (bf16[48,4224]{1,0:T(8,128)(2,1)S(1)}, bf16[48,4224]{1,0:T(8,128)(2,1)S(1)}, u32[]{:S(2)}, u32[]{:S(2)}) collective-permute-start(bf16[48,4224]{1,0:T(8,128)(2,1)S(1)} %collective-permute-done.refs_2_), channel_id=1, source_target_pairs={{0,4},{1,3},{2,6},{3,1},{4,0},{5,7},{6,2},{7,5},{8,12},{9,11},{10,... | collective-permute-start | bytes 1216520 | tf_op jit(solution)/shard_map/ppermute | solution.py:37
  41.6 14.7 %collective-permute-start.15 = (bf16[48,4224]{1,0:T(8,128)(2,1)S(1)}, bf16[48,4224]{1,0:T(8,128)(2,1)S(1)}, u32[]{:S(2)}, u32[]{:S(2)}) collective-permute-start(bf16[48,4224]{1,0:T(8,128)(2,1)S(1)} %collective-permute-done.14.refs_1_), channel_id=1, source_target_pairs={{0,2},{1,5},{2,0},{3,7},{4,6},{5,1},{6,4},{7,3},{8,10},{9,13},{10,... | collective-permute-start | bytes 1216520 | tf_op jit(solution)/shard_map/ppermute | solution.py:37
  42.9 6.8 %copy-start = (bf16[1,2048,768]{2,1,0:T(8,128)(2,1)S(1)}, bf16[1,2048,768]{2,1,0:T(8,128)(2,1)}, u32[]{:S(2)}) copy-start(bf16[1,2048,768]{2,1,0:T(8,128)(2,1)} %get-tuple-element.60) | copy-start | bytes 9437188
  46.9 17.9 %collective-permute-start.9 = (bf16[48,4224]{1,0:T(8,128)(2,1)S(1)}, bf16[48,4224]{1,0:T(8,128)(2,1)S(1)}, u32[]{:S(2)}, u32[]{:S(2)}) collective-permute-start(bf16[48,4224]{1,0:T(8,128)(2,1)S(1)} %collective-permute-done.7.refs_1_), channel_id=1, source_target_pairs={{0,4},{1,3},{2,6},{3,1},{4,0},{5,7},{6,2},{7,5},{8,12},{9,11},{10,... | collective-permute-start | bytes 1216520 | tf_op jit(solution)/shard_map/ppermute | solution.py:37
  47.7 18.8 %collective-permute-start.22 = (bf16[48,4224]{1,0:T(8,128)(2,1)S(1)}, bf16[48,4224]{1,0:T(8,128)(2,1)S(1)}, u32[]{:S(2)}, u32[]{:S(2)}) collective-permute-start(bf16[48,4224]{1,0:T(8,128)(2,1)S(1)} %collective-permute-done.21.refs_1_), channel_id=1, source_target_pairs={{0,2},{1,5},{2,0},{3,7},{4,6},{5,1},{6,4},{7,3},{8,10},{9,13},{10,... | collective-permute-start | bytes 1216520 | tf_op jit(solution)/shard_map/ppermute | solution.py:37
  49.2 17.8 %collective-permute-start.10 = (bf16[48,4224]{1,0:T(8,128)(2,1)S(1)}, bf16[48,4224]{1,0:T(8,128)(2,1)S(1)}, u32[]{:S(2)}, u32[]{:S(2)}) collective-permute-start(bf16[48,4224]{1,0:T(8,128)(2,1)S(1)} %collective-permute-done.8.refs_2_), channel_id=1, source_target_pairs={{0,4},{1,3},{2,6},{3,1},{4,0},{5,7},{6,2},{7,5},{8,12},{9,11},{10,... | collective-permute-start | bytes 1216520 | tf_op jit(solution)/shard_map/ppermute | solution.py:37
  54.8 20.2 %collective-permute-start.16 = (bf16[48,4224]{1,0:T(8,128)(2,1)S(1)}, bf16[48,4224]{1,0:T(8,128)(2,1)S(1)}, u32[]{:S(2)}, u32[]{:S(2)}) collective-permute-start(bf16[48,4224]{1,0:T(8,128)(2,1)S(1)} %collective-permute-done.14.refs_1_), channel_id=1, source_target_pairs={{0,4},{1,3},{2,6},{3,1},{4,0},{5,7},{6,2},{7,5},{8,12},{9,11},{10,... | collective-permute-start | bytes 1216520 | tf_op jit(solution)/shard_map/ppermute | solution.py:37
  56.3 18.7 %collective-permute-start.17 = (bf16[48,4224]{1,0:T(8,128)(2,1)S(1)}, bf16[48,4224]{1,0:T(8,128)(2,1)S(1)}, u32[]{:S(2)}, u32[]{:S(2)}) collective-permute-start(bf16[48,4224]{1,0:T(8,128)(2,1)S(1)} %collective-permute-done.15.refs_2_), channel_id=1, source_target_pairs={{0,4},{1,3},{2,6},{3,1},{4,0},{5,7},{6,2},{7,5},{8,12},{9,11},{10,... | collective-permute-start | bytes 1216520 | tf_op jit(solution)/shard_map/ppermute | solution.py:37
  64.9 18.2 %collective-permute-start.23 = (bf16[48,4224]{1,0:T(8,128)(2,1)S(1)}, bf16[48,4224]{1,0:T(8,128)(2,1)S(1)}, u32[]{:S(2)}, u32[]{:S(2)}) collective-permute-start(bf16[48,4224]{1,0:T(8,128)(2,1)S(1)} %collective-permute-done.21.refs_1_), channel_id=1, source_target_pairs={{0,4},{1,3},{2,6},{3,1},{4,0},{5,7},{6,2},{7,5},{8,12},{9,11},{10,... | collective-permute-start | bytes 1216520 | tf_op jit(solution)/shard_map/ppermute | solution.py:37
  66.4 16.6 %collective-permute-start.24 = (bf16[48,4224]{1,0:T(8,128)(2,1)S(1)}, bf16[48,4224]{1,0:T(8,128)(2,1)S(1)}, u32[]{:S(2)}, u32[]{:S(2)}) collective-permute-start(bf16[48,4224]{1,0:T(8,128)(2,1)S(1)} %collective-permute-done.22.refs_2_), channel_id=1, source_target_pairs={{0,4},{1,3},{2,6},{3,1},{4,0},{5,7},{6,2},{7,5},{8,12},{9,11},{10,... | collective-permute-start | bytes 1216520 | tf_op jit(solution)/shard_map/ppermute | solution.py:37
  92.7 53.6 %collective-permute-start.30 = (bf16[384,2048]{1,0:T(8,128)(2,1)S(1)}, bf16[384,2048]{1,0:T(8,128)(2,1)S(1)}, u32[]{:S(2)}, u32[]{:S(2)}) collective-permute-start(bf16[384,2048]{1,0:T(8,128)(2,1)S(1)} %convolution_convert_fusion), channel_id=1, source_target_pairs={{0,1},{1,0},{2,3},{3,2},{4,5},{5,4},{6,7},{7,6},{8,9},{9,8},{10,11... | collective-permute-start | bytes 4718600 | tf_op jit(solution)/shard_map/ppermute | solution.py:37
  92.8 7.8 %collective-permute-start.11 = (bf16[96,2048]{1,0:T(8,128)(2,1)S(1)}, bf16[96,2048]{1,0:T(8,128)(2,1)S(1)}, u32[]{:S(2)}, u32[]{:S(2)}) collective-permute-start(bf16[96,2048]{1,0:T(8,128)(2,1)S(1)} %get-tuple-element.40), channel_id=1, source_target_pairs={{0,4},{1,3},{2,6},{3,1},{4,0},{5,7},{6,2},{7,5},{8,12},{9,11},{10,... | collective-permute-start | bytes 1179656 | tf_op jit(solution)/shard_map/ppermute | solution.py:37
  96.3 52.7 %collective-permute-start.29 = (bf16[2048,384]{1,0:T(8,128)(2,1)S(1)}, bf16[2048,384]{1,0:T(8,128)(2,1)S(1)}, u32[]{:S(2)}, u32[]{:S(2)}) collective-permute-start(bf16[2048,384]{1,0:T(8,128)(2,1)S(1)} %convolution_convert_fusion.1), channel_id=1, source_target_pairs={{0,1},{1,0},{2,3},{3,2},{4,5},{5,4},{6,7},{7,6},{8,9},{9,8},{10,11... | collective-permute-start | bytes 4718600 | tf_op jit(solution)/shard_map/ppermute | solution.py:37
  96.3 8.5 %collective-permute-start.18 = (bf16[96,2048]{1,0:T(8,128)(2,1)S(1)}, bf16[96,2048]{1,0:T(8,128)(2,1)S(1)}, u32[]{:S(2)}, u32[]{:S(2)}) collective-permute-start(bf16[96,2048]{1,0:T(8,128)(2,1)S(1)} %get-tuple-element.47), channel_id=1, source_target_pairs={{0,4},{1,3},{2,6},{3,1},{4,0},{5,7},{6,2},{7,5},{8,12},{9,11},{10,... | collective-permute-start | bytes 1179656 | tf_op jit(solution)/shard_map/ppermute | solution.py:37
  97.0 14.1 %collective-permute-start.25 = (bf16[96,2048]{1,0:T(8,128)(2,1)S(1)}, bf16[96,2048]{1,0:T(8,128)(2,1)S(1)}, u32[]{:S(2)}, u32[]{:S(2)}) collective-permute-start(bf16[96,2048]{1,0:T(8,128)(2,1)S(1)} %get-tuple-element.54), channel_id=1, source_target_pairs={{0,4},{1,3},{2,6},{3,1},{4,0},{5,7},{6,2},{7,5},{8,12},{9,11},{10,... | collective-permute-start | bytes 1179656 | tf_op jit(solution)/shard_map/ppermute | solution.py:37
  100.6 16.9 %collective-permute-start.5 = (bf16[96,2048]{1,0:T(8,128)(2,1)S(1)}, bf16[96,2048]{1,0:T(8,128)(2,1)S(1)}, u32[]{:S(2)}, u32[]{:S(2)}) collective-permute-start(bf16[96,2048]{1,0:T(8,128)(2,1)S(1)} %get-tuple-element.33), channel_id=1, source_target_pairs={{0,4},{1,3},{2,6},{3,1},{4,0},{5,7},{6,2},{7,5},{8,12},{9,11},{10,... | collective-permute-start | bytes 1179656 | tf_op jit(solution)/shard_map/ppermute | solution.py:37
  104.8 14.1 %collective-permute-start.12 = (bf16[48,2048]{1,0:T(8,128)(2,1)S(1)}, bf16[48,2048]{1,0:T(8,128)(2,1)S(1)}, u32[]{:S(2)}, u32[]{:S(2)}) collective-permute-start(bf16[48,2048]{1,0:T(8,128)(2,1)S(1)} %slice.116), channel_id=1, source_target_pairs={{0,2},{1,5},{2,0},{3,7},{4,6},{5,1},{6,4},{7,3},{8,10},{9,13},{10,... | collective-permute-start | bytes 589832 | tf_op jit(solution)/shard_map/ppermute | solution.py:37
  111.1 8.7 %collective-permute-start.19 = (bf16[48,2048]{1,0:T(8,128)(2,1)S(1)}, bf16[48,2048]{1,0:T(8,128)(2,1)S(1)}, u32[]{:S(2)}, u32[]{:S(2)}) collective-permute-start(bf16[48,2048]{1,0:T(8,128)(2,1)S(1)} %slice.115), channel_id=1, source_target_pairs={{0,2},{1,5},{2,0},{3,7},{4,6},{5,1},{6,4},{7,3},{8,10},{9,13},{10,... | collective-permute-start | bytes 589832 | tf_op jit(solution)/shard_map/ppermute | solution.py:37
  117.5 13.2 %collective-permute-start.26 = (bf16[48,2048]{1,0:T(8,128)(2,1)S(1)}, bf16[48,2048]{1,0:T(8,128)(2,1)S(1)}, u32[]{:S(2)}, u32[]{:S(2)}) collective-permute-start(bf16[48,2048]{1,0:T(8,128)(2,1)S(1)} %slice.114), channel_id=1, source_target_pairs={{0,2},{1,5},{2,0},{3,7},{4,6},{5,1},{6,4},{7,3},{8,10},{9,13},{10,... | collective-permute-start | bytes 589832 | tf_op jit(solution)/shard_map/ppermute | solution.py:37
  118.9 11.9 %collective-permute-start.6 = (bf16[48,2048]{1,0:T(8,128)(2,1)S(1)}, bf16[48,2048]{1,0:T(8,128)(2,1)S(1)}, u32[]{:S(2)}, u32[]{:S(2)}) collective-permute-start(bf16[48,2048]{1,0:T(8,128)(2,1)S(1)} %slice.117), channel_id=1, source_target_pairs={{0,2},{1,5},{2,0},{3,7},{4,6},{5,1},{6,4},{7,3},{8,10},{9,13},{10,... | collective-permute-start | bytes 589832 | tf_op jit(solution)/shard_map/ppermute | solution.py:37
  119.8 16.8 %collective-permute-start.13 = (bf16[48,2048]{1,0:T(8,128)(2,1)S(1)}, bf16[48,2048]{1,0:T(8,128)(2,1)S(1)}, u32[]{:S(2)}, u32[]{:S(2)}) collective-permute-start(bf16[48,2048]{1,0:T(8,128)(2,1)S(1)} %fusion.17), channel_id=1, source_target_pairs={{0,24},{1,25},{2,26},{3,27},{4,28},{5,29},{6,30},{7,31},{8,0},{9,1... | collective-permute-start | bytes 589832 | tf_op jit(solution)/shard_map/ppermute | solution.py:37
  130.7 14.9 %collective-permute-start.20 = (bf16[48,2048]{1,0:T(8,128)(2,1)S(1)}, bf16[48,2048]{1,0:T(8,128)(2,1)S(1)}, u32[]{:S(2)}, u32[]{:S(2)}) collective-permute-start(bf16[48,2048]{1,0:T(8,128)(2,1)S(1)} %fusion.16), channel_id=1, source_target_pairs={{0,16},{1,17},{2,18},{3,19},{4,20},{5,21},{6,22},{7,23},{8,24},{9,... | collective-permute-start | bytes 589832 | tf_op jit(solution)/shard_map/ppermute | solution.py:37
  130.8 14.7 %collective-permute-start.27 = (bf16[48,2048]{1,0:T(8,128)(2,1)S(1)}, bf16[48,2048]{1,0:T(8,128)(2,1)S(1)}, u32[]{:S(2)}, u32[]{:S(2)}) collective-permute-start(bf16[48,2048]{1,0:T(8,128)(2,1)S(1)} %fusion.15), channel_id=1, source_target_pairs={{0,8},{1,9},{2,10},{3,11},{4,12},{5,13},{6,14},{7,15},{8,16},{9,17... | collective-permute-start | bytes 589832 | tf_op jit(solution)/shard_map/ppermute | solution.py:37
  136.5 15.5 %collective-permute-start.28 = (bf16[2048,384]{1,0:T(8,128)(2,1)S(1)}, bf16[2048,384]{1,0:T(8,128)(2,1)S(1)}, u32[]{:S(2)}, u32[]{:S(2)}) collective-permute-start(bf16[2048,384]{1,0:T(8,128)(2,1)S(1)} %convolution_convert_fusion.2), channel_id=1, source_target_pairs={{0,1},{1,0},{2,3},{3,2},{4,5},{5,4},{6,7},{7,6},{8,9},{9,8},{10,11... | collective-permute-start | bytes 4718600 | tf_op jit(solution)/shard_map/ppermute | solution.py:37

commit v2 on v1

--- a/solution.py
+++ b/solution.py
@@ -115,8 +115,10 @@
     mine = (lax.axis_index("rep") * lax.axis_size("exp") + lax.axis_index("exp")) // 2
 
     in_own = jnp.concatenate([gate_weight[0], up_weight[0]], axis=1)
-    in_mats = jnp.stack([in_own, move(in_own, OTHER_CORE)])
-    down_mats = jnp.stack([down_weight[0], move(down_weight[0], OTHER_CORE)])
+    in_other = move(in_own, OTHER_CORE)
+    down_other = move(down_weight[0], OTHER_CORE)
+    in_mats = jnp.stack([in_own, in_other])
+    down_mats = jnp.stack([down_weight[0], down_other])
 
     chosen = expert_ids[:, :, None] == jnp.arange(experts, dtype=jnp.int32)
     dense = jnp.sum(jnp.where(chosen, gate_probs[:, :, None], 0.0), axis=1)
@@ -145,11 +147,14 @@
 
     def grads(part):
         pairs = ((all_in, all_gate[part]), (all_in, all_up[part]), (all_hidden[part], all_scaled))
-        return [lax.dot_general(a, b, FIRST, preferred_element_type=F32) for a, b in pairs]
-
-    other = [value.astype(B16) for value in grads(1)]
-    arrived = [move(value, OTHER_CORE) for value in other]
-    summed = [(here + there.astype(F32)).astype(B16)[None] for here, there in zip(grads(0), arrived)]
+        return [functools.partial(lax.dot_general, a, b, FIRST, preferred_element_type=F32) for a, b in pairs]
+
+    arrived, summed = [], []
+    for other in grads(1):
+        value = other().astype(B16)
+        arrived.append(move(value, OTHER_CORE))
+    for i, own in enumerate(grads(0)):
+        summed.append((own() + arrived[i].astype(F32)).astype(B16)[None])
     return (token_grad, *summed)
 
 

time: 155 us -> 155 us (level)
  no operation moved by 1% of the time
where the time goes in v2:
time: 155 us
  waiting for transfers between devices  46.9 us (30%)
  starting transfers between devices  45.4 us (29%)
  Pallas kernels  32.3 us (21%)
  other arithmetic  15.4 us (10%)
  matrix products  13.9 us (9%)
    ppermute x31, waiting for transfers between devices, move(): return lax.ppermute(value, AXES, pairs)  46.9 us
    ppermute x31, starting transfers between devices, move(): return lax.ppermute(value, AXES, pairs)  45.4 us
    pallas_call x4, Pallas kernels, chunk_call(): pl.pallas_call(functools.partial(chunk_kernel, features, half, rows), gri...  32.3 us
    another operation x2, other arithmetic, dense_device(): in_mats = jnp.stack([in_own, in_other])  10 us
    dot_general x3, matrix products, dense_device(): summed.append((own() + arrived[i].astype(F32)).astype(B16)[None])  8.72 us
    dot_general x3, matrix products, dense_device(): value = other().astype(B16)  5.16 us
    another operation x1, other arithmetic, dense_device(): down_mats = jnp.stack([down_weight[0], down_other])  4.01 us
  transfers between devices with their start and end apart: 31, of which 8 were waited for; matrix products, arithmetic and copies ran while one was open for 13% of the time, Pallas kernels for 16%

profile of v2, /device:TPU:0, one launch (start us, length us, event | category | flops | bytes accessed | tf_op | source)
XLA Modules:
  0.0 155.1 jit_solution(8683709136939118941)
XLA Ops:
  0.7 4.9 %fusion.28 = (bf16[1,2048,768]{2,1,0:T(8,128)(2,1)}, bf16[2048,768]{1,0:T(8,128)(2,1)}) fusion(bf16[2048,384]{1,0:T(8,128)(2,1)} %bitcast.37, bf16[2048,384]{1,0:T(8,128)(2,1)} %bitcast.38), kind=kLoop, calls=%fused_computation.57 | loop fusion | flops 6291456 | bytes 9437184 | tf_op jit(solution)/shard_map/stack | solution.py:120
  5.6 0.5 collective-permute-start.3
  6.1 0.0 collective-permute-start.4
  6.1 0.1 copy.31
  6.2 0.1 copy.30
  6.3 0.1 fusion.27
  6.4 3.0 %collective-permute-start = (bf16[48,4224]{1,0:T(8,128)(2,1)S(1)}, bf16[48,4224]{1,0:T(8,128)(2,1)S(1)}, u32[]{:S(2)}, u32[]{:S(2)}) collective-permute-start(bf16[48,4224]{1,0:T(8,128)(2,1)S(1)} %pad_maximum_fusion.3.refs_1_), channel_id=1, source_target_pairs={{0,2},{1,5},{2,0},{3,7},{4,6},{5,1},{6,4},{7,3},{8,10},{9,13},{10,... | collective-permute-start | bytes 1216520 | tf_op jit(solution)/shard_map/ppermute | solution.py:37
  9.5 1.5 collective-permute-start.1
  11.0 1.6 %collective-permute-start.7 = (bf16[48,4224]{1,0:T(8,128)(2,1)S(1)}, bf16[48,4224]{1,0:T(8,128)(2,1)S(1)}, u32[]{:S(2)}, u32[]{:S(2)}) collective-permute-start(bf16[48,4224]{1,0:T(8,128)(2,1)S(1)} %pad_maximum_fusion.3.refs_1_), channel_id=1, source_target_pairs={{0,8},{1,9},{2,10},{3,11},{4,12},{5,13},{6,14},{7,15},{8,16},{9,17... | collective-permute-start | bytes 1216520 | tf_op jit(solution)/shard_map/ppermute | solution.py:37
  12.6 6.4 %collective-permute-done.refs_2_ = bf16[48,4224]{1,0:T(8,128)(2,1)S(1)} collective-permute-done((bf16[48,4224]{1,0:T(8,128)(2,1)S(1)}, bf16[48,4224]{1,0:T(8,128)(2,1)S(1)}, u32[]{:S(2)}, u32[]{:S(2)}) %collective-permute-start) | collective-permute-done | bytes 405536 | tf_op jit(solution)/shard_map/ppermute | solution.py:37
  19.0 3.6 %collective-permute-start.14 = (bf16[48,4224]{1,0:T(8,128)(2,1)S(1)}, bf16[48,4224]{1,0:T(8,128)(2,1)S(1)}, u32[]{:S(2)}, u32[]{:S(2)}) collective-permute-start(bf16[48,4224]{1,0:T(8,128)(2,1)S(1)} %pad_maximum_fusion.3.refs_1_), channel_id=1, source_target_pairs={{0,16},{1,17},{2,18},{3,19},{4,20},{5,21},{6,22},{7,23},{8,24},{9,... | collective-permute-start | bytes 1216520 | tf_op jit(solution)/shard_map/ppermute | solution.py:37
  22.5 0.0 collective-permute-done.1.refs_3_
  22.5 1.3 collective-permute-start.21
  23.9 1.3 collective-permute-done.7.refs_1_
  25.1 0.2 collective-permute-start.8
  25.4 15.7 %collective-permute-done.14.refs_1_ = bf16[48,4224]{1,0:T(8,128)(2,1)S(1)} collective-permute-done((bf16[48,4224]{1,0:T(8,128)(2,1)S(1)}, bf16[48,4224]{1,0:T(8,128)(2,1)S(1)}, u32[]{:S(2)}, u32[]{:S(2)}) %collective-permute-start.14) | collective-permute-done | bytes 405536 | tf_op jit(solution)/shard_map/ppermute | solution.py:37
  41.1 0.5 collective-permute-start.2
  41.6 0.0 collective-permute-done.4
  41.6 1.3 collective-permute-start.15
  42.9 4.0 %pad_maximum_fusion.2.refs_6_ = bf16[2,384,2048]{2,1,0:T(8,128)(2,1)} fusion(bf16[1,384,2048]{2,1,0:T(8,128)(2,1)} %bitcast.5, bf16[1,384,2048]{2,1,0:T(8,128)(2,1)} %param.13), kind=kLoop, calls=%fused_computation.2 | loop fusion | flops 1572864 | bytes 6291456 | tf_op jit(solution)/shard_map/stack | solution.py:121
  46.9 0.7 collective-permute-start.9
  47.7 1.5 collective-permute-start.22
  49.2 0.5 collective-permute-start.10
  49.7 5.1 %pad_maximum_fusion.refs_5_ = bf16[2,2048,768]{2,1,0:T(8,128)(2,1)} fusion(bf16[1,2048,768]{2,1,0:T(8,128)(2,1)} %bitcast.3, bf16[1,2048,768]{2,1,0:T(8,128)(2,1)S(1)} %copy-done), kind=kLoop, calls=%fused_computation | loop fusion | flops 3145728 | bytes 12582912 | tf_op jit(solution)/shard_map/stack | solution.py:120
  54.8 1.5 collective-permute-start.16
  56.3 0.5 collective-permute-start.17
  56.8 8.0 %shard_map.102 = (bf16[768,2048]{1,0:T(8,128)(2,1)S(1)}, bf16[768,2048]{1,0:T(8,128)(2,1)S(1)}, bf16[2,768,384]{2,1,0:T(8,128)(2,1)S(1)}, bf16[2,768,384]{2,1,0:...) custom-call(f32[1,128]{1,0:T(1,128)S(1)} %and_convert_fusion.refs_0_, ...), custom_call_target="tpu_custom_call" | custom-call | flops 3019898880 | bytes 25165824 | tf_op jit(solution)/shard_map/pallas_call | solution.py:95
  64.9 1.6 %collective-permute-start.23 = (bf16[48,4224]{1,0:T(8,128)(2,1)S(1)}, bf16[48,4224]{1,0:T(8,128)(2,1)S(1)}, u32[]{:S(2)}, u32[]{:S(2)}) collective-permute-start(bf16[48,4224]{1,0:T(8,128)(2,1)S(1)} %collective-permute-done.21.refs_1_), channel_id=1, source_target_pairs={{0,4},{1,3},{2,6},{3,1},{4,0},{5,7},{6,2},{7,5},{8,12},{9,11},{10,... | collective-permute-start | bytes 1216520 | tf_op jit(solution)/shard_map/ppermute | solution.py:37
  66.4 0.5 collective-permute-start.24
  67.0 8.0 %shard_map.103 = (bf16[768,2048]{1,0:T(8,128)(2,1)S(1)}, bf16[768,2048]{1,0:T(8,128)(2,1)S(1)}, bf16[2,768,384]{2,1,0:T(8,128)(2,1)S(1)}, bf16[2,768,384]{2,1,0:...) custom-call(f32[1,128]{1,0:T(1,128)S(1)} %and_convert_fusion.refs_0_, ...), custom_call_target="tpu_custom_call", output_to_operand_aliasing={{0}: (7, {}), {1}: (8, {}), {2}: (9, {}), {3}: (10, {}), {4... | custom-call | flops 3019898880 | bytes 25165824 | tf_op jit(solution)/shard_map/pallas_call | solution.py:95
  75.0 8.0 %shard_map.104 = (bf16[768,2048]{1,0:T(8,128)(2,1)S(1)}, bf16[768,2048]{1,0:T(8,128)(2,1)S(1)}, bf16[2,768,384]{2,1,0:T(8,128)(2,1)S(1)}, bf16[2,768,384]{2,1,0:...) custom-call(f32[1,128]{1,0:T(1,128)S(1)} %and_convert_fusion.refs_0_, ...), custom_call_target="tpu_custom_call", output_to_operand_aliasing={{0}: (7, {}), {1}: (8, {}), {2}: (9, {}), {3}: (10, {}), {4... | custom-call | flops 3019898880 | bytes 25165824 | tf_op jit(solution)/shard_map/pallas_call | solution.py:95
  83.1 8.2 %shard_map.105 = (bf16[768,2048]{1,0:T(8,128)(2,1)S(1)}, bf16[768,2048]{1,0:T(8,128)(2,1)S(1)}, bf16[2,768,384]{2,1,0:T(8,128)(2,1)S(1)}, bf16[2,768,384]{2,1,0:...) custom-call(f32[1,128]{1,0:T(1,128)S(1)} %and_convert_fusion.refs_0_, ...), custom_call_target="tpu_custom_call", output_to_operand_aliasing={{0}: (7, {}), {1}: (8, {}), {2}: (9, {}), {3}: (10, {}), {4... | custom-call | flops 3019898880 | bytes 25165824 | tf_op jit(solution)/shard_map/pallas_call | solution.py:95
  91.3 1.4 convolution_convert_fusion
  92.7 0.1 collective-permute-start.30
  92.8 1.6 %collective-permute-start.11 = (bf16[96,2048]{1,0:T(8,128)(2,1)S(1)}, bf16[96,2048]{1,0:T(8,128)(2,1)S(1)}, u32[]{:S(2)}, u32[]{:S(2)}) collective-permute-start(bf16[96,2048]{1,0:T(8,128)(2,1)S(1)} %get-tuple-element.40), channel_id=1, source_target_pairs={{0,4},{1,3},{2,6},{3,1},{4,0},{5,7},{6,2},{7,5},{8,12},{9,11},{10,... | collective-permute-start | bytes 1179656 | tf_op jit(solution)/shard_map/ppermute | solution.py:37
  94.4 1.9 %convolution_convert_fusion.1 = bf16[2048,384]{1,0:T(8,128)(2,1)S(1)} fusion(bf16[768,2048]{1,0:T(8,128)(2,1)S(1)} %get-tuple-element.55, bf16[2,768,384]{2,1,0:T(8,128)(2,1)S(1)} %get-tuple-element.57), kind=kOutput, calls=%fused_computation.7 | convolution fusion | flops 1208745984 | bytes 5308416 | tf_op jit(solution)/shard_map/dot_general | solution.py:154
  96.3 0.1 collective-permute-start.29
  96.3 0.7 collective-permute-start.18
  97.0 1.4 collective-permute-start.25
  98.4 2.2 %collective-permute-done.11 = bf16[96,2048]{1,0:T(8,128)(2,1)S(1)} collective-permute-done((bf16[96,2048]{1,0:T(8,128)(2,1)S(1)}, bf16[96,2048]{1,0:T(8,128)(2,1)S(1)}, u32[]{:S(2)}, u32[]{:S(2)}) %collective-permute-start.11) | collective-permute-done | bytes 393248 | tf_op jit(solution)/shard_map/ppermute | solution.py:37
  100.6 1.5 collective-permute-start.5
  102.2 0.1 convert_add_fusion.2
  102.3 2.6 %collective-permute-done.18 = bf16[96,2048]{1,0:T(8,128)(2,1)S(1)} collective-permute-done((bf16[96,2048]{1,0:T(8,128)(2,1)S(1)}, bf16[96,2048]{1,0:T(8,128)(2,1)S(1)}, u32[]{:S(2)}, u32[]{:S(2)}) %collective-permute-start.18) | collective-permute-done | bytes 393248 | tf_op jit(solution)/shard_map/ppermute | solution.py:37
  104.8 1.3 collective-permute-start.12
  106.2 0.1 convert_add_fusion.1
  106.3 4.8 %collective-permute-done.25 = bf16[96,2048]{1,0:T(8,128)(2,1)S(1)} collective-permute-done((bf16[96,2048]{1,0:T(8,128)(2,1)S(1)}, bf16[96,2048]{1,0:T(8,128)(2,1)S(1)}, u32[]{:S(2)}, u32[]{:S(2)}) %collective-permute-start.25) | collective-permute-done | bytes 393248 | tf_op jit(solution)/shard_map/ppermute | solution.py:37
  111.1 1.3 collective-permute-start.19
  112.4 0.1 convert_add_fusion
  112.5 4.9 %collective-permute-done.5 = bf16[96,2048]{1,0:T(8,128)(2,1)S(1)} collective-permute-done((bf16[96,2048]{1,0:T(8,128)(2,1)S(1)}, bf16[96,2048]{1,0:T(8,128)(2,1)S(1)}, u32[]{:S(2)}, u32[]{:S(2)}) %collective-permute-start.5) | collective-permute-done | bytes 393248 | tf_op jit(solution)/shard_map/ppermute | solution.py:37
  117.5 1.3 collective-permute-start.26
  118.8 0.1 convert_add_fusion.3
  118.9 0.8 collective-permute-start.6
  119.8 10.8 %collective-permute-start.13 = (bf16[48,2048]{1,0:T(8,128)(2,1)S(1)}, bf16[48,2048]{1,0:T(8,128)(2,1)S(1)}, u32[]{:S(2)}, u32[]{:S(2)}) collective-permute-start(bf16[48,2048]{1,0:T(8,128)(2,1)S(1)} %fusion.17), channel_id=1, source_target_pairs={{0,24},{1,25},{2,26},{3,27},{4,28},{5,29},{6,30},{7,31},{8,0},{9,1... | collective-permute-start | bytes 589832 | tf_op jit(solution)/shard_map/ppermute | solution.py:37
  130.6 0.1 fusion.16
  130.7 0.1 collective-permute-start.20
  130.8 0.1 fusion.15
  130.8 3.8 %collective-permute-start.27 = (bf16[48,2048]{1,0:T(8,128)(2,1)S(1)}, bf16[48,2048]{1,0:T(8,128)(2,1)S(1)}, u32[]{:S(2)}, u32[]{:S(2)}) collective-permute-start(bf16[48,2048]{1,0:T(8,128)(2,1)S(1)} %fusion.15), channel_id=1, source_target_pairs={{0,8},{1,9},{2,10},{3,11},{4,12},{5,13},{6,14},{7,15},{8,16},{9,17... | collective-permute-start | bytes 589832 | tf_op jit(solution)/shard_map/ppermute | solution.py:37
  134.6 1.9 %convolution_convert_fusion.2 = bf16[2048,384]{1,0:T(8,128)(2,1)S(1)} fusion(bf16[768,2048]{1,0:T(8,128)(2,1)S(1)} %get-tuple-element.55, bf16[2,768,384]{2,1,0:T(8,128)(2,1)S(1)} %get-tuple-element.56), kind=kOutput, calls=%fused_computation.8 | convolution fusion | flops 1208745984 | bytes 5308416 | tf_op jit(solution)/shard_map/dot_general | solution.py:154
  136.5 0.1 collective-permute-start.28
  136.6 8.9 %collective-permute-done.20 = bf16[48,2048]{1,0:T(8,128)(2,1)S(1)} collective-permute-done((bf16[48,2048]{1,0:T(8,128)(2,1)S(1)}, bf16[48,2048]{1,0:T(8,128)(2,1)S(1)}, u32[]{:S(2)}, u32[]{:S(2)}) %collective-permute-start.20) | collective-permute-done | bytes 196640 | tf_op jit(solution)/shard_map/ppermute | solution.py:37
  145.5 0.8 fusion.21
  146.3 2.6 %fusion.2 = bf16[1,384,2048]{2,1,0:T(8,128)(2,1)} fusion(bf16[384,2048]{1,0:T(8,128)(2,1)S(1)} %collective-permute-done.30, bf16[768,2048]{1,0:T(8,128)(2,1)S(1)} %get-tuple-element.59, bf16[2,768,384]{2,1,0:T(8,128)(2,1)S(1)} %get-tuple-element.58), kind=kOutput, calls=%fused_computation.11 | convolution fusion | flops 1210318848 | bytes 6881280 | tf_op jit(solution)/shard_map/dot_general | solution.py:157
  149.0 3.1 %fusion.1 = bf16[1,2048,384]{2,1,0:T(8,128)(2,1)} fusion(bf16[2048,384]{1,0:T(8,128)(2,1)S(1)} %collective-permute-done.29, bf16[768,2048]{1,0:T(8,128)(2,1)S(1)} %get-tuple-element.55, bf16[2,768,384]{2,1,0:T(8,128)(2,1)S(1)} %get-tuple-element.57), kind=kOutput, calls=%fused_computation.10 | convolution fusion | flops 1210318848 | bytes 6881280 | tf_op jit(solution)/shard_map/dot_general | solution.py:157
  152.0 3.0 %fusion = bf16[1,2048,384]{2,1,0:T(8,128)(2,1)} fusion(bf16[2048,384]{1,0:T(8,128)(2,1)S(1)} %collective-permute-done.28, bf16[768,2048]{1,0:T(8,128)(2,1)S(1)} %get-tuple-element.55, bf16[2,768,384]{2,1,0:T(8,128)(2,1)S(1)} %get-tuple-element.56), kind=kOutput, calls=%fused_computation.9 | convolution fusion | flops 1210318848 | bytes 6881280 | tf_op jit(solution)/shard_map/dot_general | solution.py:157
  (41 shorter events, 0.3 us)
Async XLA Ops:
  0.6 5.5 %copy-start.3 = (f32[48,8]{0,1:T(8,128)S(1)}, f32[48,8]{0,1:T(8,128)}, u32[]{:S(2)}) copy-start(f32[48,8]{0,1:T(8,128)} %param.10) | copy-start | bytes 4612
  0.6 5.5 %copy-start.4 = (s32[48,8]{0,1:T(8,128)S(1)}, s32[48,8]{0,1:T(8,128)}, u32[]{:S(2)}) copy-start(s32[48,8]{0,1:T(8,128)} %param.9) | copy-start | bytes 4612
  0.7 5.7 %copy-start.1 = (bf16[48,2048]{1,0:T(8,128)(2,1)S(1)}, bf16[48,2048]{1,0:T(8,128)(2,1)}, u32[]{:S(2)}) copy-start(bf16[48,2048]{1,0:T(8,128)(2,1)} %param.8) | copy-start | bytes 589828
  0.7 5.7 %copy-start.2 = (bf16[48,2048]{1,0:T(8,128)(2,1)S(1)}, bf16[48,2048]{1,0:T(8,128)(2,1)}, u32[]{:S(2)}) copy-start(bf16[48,2048]{1,0:T(8,128)(2,1)} %param.7) | copy-start | bytes 589828
  5.6 43.6 %collective-permute-start.3 = (bf16[2048,768]{1,0:T(8,128)(2,1)}, bf16[2048,768]{1,0:T(8,128)(2,1)}, u32[]{:S(2)}, u32[]{:S(2)}) collective-permute-start(bf16[2048,768]{1,0:T(8,128)(2,1)} %get-tuple-element.61), channel_id=1, source_target_pairs={{0,1},{1,0},{2,3},{3,2},{4,5},{5,4},{6,7},{7,6},{8,9},{9,8},{10,11... | collective-permute-start | bytes 9437192 | tf_op jit(solution)/shard_map/ppermute | solution.py:37
  6.1 35.5 %collective-permute-start.4 = (bf16[384,2048]{1,0:T(8,128)(2,1)}, bf16[384,2048]{1,0:T(8,128)(2,1)}, u32[]{:S(2)}, u32[]{:S(2)}) collective-permute-start(bf16[384,2048]{1,0:T(8,128)(2,1)} %bitcast.4), channel_id=1, source_target_pairs={{0,1},{1,0},{2,3},{3,2},{4,5},{5,4},{6,7},{7,6},{8,9},{9,8},{10,11... | collective-permute-start | bytes 4718600 | tf_op jit(solution)/shard_map/ppermute | solution.py:37
  6.4 12.5 %collective-permute-start = (bf16[48,4224]{1,0:T(8,128)(2,1)S(1)}, bf16[48,4224]{1,0:T(8,128)(2,1)S(1)}, u32[]{:S(2)}, u32[]{:S(2)}) collective-permute-start(bf16[48,4224]{1,0:T(8,128)(2,1)S(1)} %pad_maximum_fusion.3.refs_1_), channel_id=1, source_target_pairs={{0,2},{1,5},{2,0},{3,7},{4,6},{5,1},{6,4},{7,3},{8,10},{9,13},{10,... | collective-permute-start | bytes 1216520 | tf_op jit(solution)/shard_map/ppermute | solution.py:37
  9.5 13.1 %collective-permute-start.1 = (bf16[48,4224]{1,0:T(8,128)(2,1)S(1)}, bf16[48,4224]{1,0:T(8,128)(2,1)S(1)}, u32[]{:S(2)}, u32[]{:S(2)}) collective-permute-start(bf16[48,4224]{1,0:T(8,128)(2,1)S(1)} %pad_maximum_fusion.3.refs_1_), channel_id=1, source_target_pairs={{0,4},{1,3},{2,6},{3,1},{4,0},{5,7},{6,2},{7,5},{8,12},{9,11},{10,... | collective-permute-start | bytes 1216520 | tf_op jit(solution)/shard_map/ppermute | solution.py:37
  11.0 14.2 %collective-permute-start.7 = (bf16[48,4224]{1,0:T(8,128)(2,1)S(1)}, bf16[48,4224]{1,0:T(8,128)(2,1)S(1)}, u32[]{:S(2)}, u32[]{:S(2)}) collective-permute-start(bf16[48,4224]{1,0:T(8,128)(2,1)S(1)} %pad_maximum_fusion.3.refs_1_), channel_id=1, source_target_pairs={{0,8},{1,9},{2,10},{3,11},{4,12},{5,13},{6,14},{7,15},{8,16},{9,17... | collective-permute-start | bytes 1216520 | tf_op jit(solution)/shard_map/ppermute | solution.py:37
  19.0 22.1 %collective-permute-start.14 = (bf16[48,4224]{1,0:T(8,128)(2,1)S(1)}, bf16[48,4224]{1,0:T(8,128)(2,1)S(1)}, u32[]{:S(2)}, u32[]{:S(2)}) collective-permute-start(bf16[48,4224]{1,0:T(8,128)(2,1)S(1)} %pad_maximum_fusion.3.refs_1_), channel_id=1, source_target_pairs={{0,16},{1,17},{2,18},{3,19},{4,20},{5,21},{6,22},{7,23},{8,24},{9,... | collective-permute-start | bytes 1216520 | tf_op jit(solution)/shard_map/ppermute | solution.py:37
  22.5 24.4 %collective-permute-start.21 = (bf16[48,4224]{1,0:T(8,128)(2,1)S(1)}, bf16[48,4224]{1,0:T(8,128)(2,1)S(1)}, u32[]{:S(2)}, u32[]{:S(2)}) collective-permute-start(bf16[48,4224]{1,0:T(8,128)(2,1)S(1)} %pad_maximum_fusion.3.refs_1_), channel_id=1, source_target_pairs={{0,24},{1,25},{2,26},{3,27},{4,28},{5,29},{6,30},{7,31},{8,0},{9,1... | collective-permute-start | bytes 1216520 | tf_op jit(solution)/shard_map/ppermute | solution.py:37
  25.1 22.5 %collective-permute-start.8 = (bf16[48,4224]{1,0:T(8,128)(2,1)S(1)}, bf16[48,4224]{1,0:T(8,128)(2,1)S(1)}, u32[]{:S(2)}, u32[]{:S(2)}) collective-permute-start(bf16[48,4224]{1,0:T(8,128)(2,1)S(1)} %collective-permute-done.7.refs_1_), channel_id=1, source_target_pairs={{0,2},{1,5},{2,0},{3,7},{4,6},{5,1},{6,4},{7,3},{8,10},{9,13},{10,... | collective-permute-start | bytes 1216520 | tf_op jit(solution)/shard_map/ppermute | solution.py:37
  41.1 13.7 %collective-permute-start.2 = (bf16[48,4224]{1,0:T(8,128)(2,1)S(1)}, bf16[48,4224]{1,0:T(8,128)(2,1)S(1)}, u32[]{:S(2)}, u32[]{:S(2)}) collective-permute-start(bf16[48,4224]{1,0:T(8,128)(2,1)S(1)} %collective-permute-done.refs_2_), channel_id=1, source_target_pairs={{0,4},{1,3},{2,6},{3,1},{4,0},{5,7},{6,2},{7,5},{8,12},{9,11},{10,... | collective-permute-start | bytes 1216520 | tf_op jit(solution)/shard_map/ppermute | solution.py:37
  41.6 14.7 %collective-permute-start.15 = (bf16[48,4224]{1,0:T(8,128)(2,1)S(1)}, bf16[48,4224]{1,0:T(8,128)(2,1)S(1)}, u32[]{:S(2)}, u32[]{:S(2)}) collective-permute-start(bf16[48,4224]{1,0:T(8,128)(2,1)S(1)} %collective-permute-done.14.refs_1_), channel_id=1, source_target_pairs={{0,2},{1,5},{2,0},{3,7},{4,6},{5,1},{6,4},{7,3},{8,10},{9,13},{10,... | collective-permute-start | bytes 1216520 | tf_op jit(solution)/shard_map/ppermute | solution.py:37
  42.9 6.8 %copy-start = (bf16[1,2048,768]{2,1,0:T(8,128)(2,1)S(1)}, bf16[1,2048,768]{2,1,0:T(8,128)(2,1)}, u32[]{:S(2)}) copy-start(bf16[1,2048,768]{2,1,0:T(8,128)(2,1)} %get-tuple-element.60) | copy-start | bytes 9437188
  46.9 17.9 %collective-permute-start.9 = (bf16[48,4224]{1,0:T(8,128)(2,1)S(1)}, bf16[48,4224]{1,0:T(8,128)(2,1)S(1)}, u32[]{:S(2)}, u32[]{:S(2)}) collective-permute-start(bf16[48,4224]{1,0:T(8,128)(2,1)S(1)} %collective-permute-done.7.refs_1_), channel_id=1, source_target_pairs={{0,4},{1,3},{2,6},{3,1},{4,0},{5,7},{6,2},{7,5},{8,12},{9,11},{10,... | collective-permute-start | bytes 1216520 | tf_op jit(solution)/shard_map/ppermute | solution.py:37
  47.7 18.8 %collective-permute-start.22 = (bf16[48,4224]{1,0:T(8,128)(2,1)S(1)}, bf16[48,4224]{1,0:T(8,128)(2,1)S(1)}, u32[]{:S(2)}, u32[]{:S(2)}) collective-permute-start(bf16[48,4224]{1,0:T(8,128)(2,1)S(1)} %collective-permute-done.21.refs_1_), channel_id=1, source_target_pairs={{0,2},{1,5},{2,0},{3,7},{4,6},{5,1},{6,4},{7,3},{8,10},{9,13},{10,... | collective-permute-start | bytes 1216520 | tf_op jit(solution)/shard_map/ppermute | solution.py:37
  49.2 17.8 %collective-permute-start.10 = (bf16[48,4224]{1,0:T(8,128)(2,1)S(1)}, bf16[48,4224]{1,0:T(8,128)(2,1)S(1)}, u32[]{:S(2)}, u32[]{:S(2)}) collective-permute-start(bf16[48,4224]{1,0:T(8,128)(2,1)S(1)} %collective-permute-done.8.refs_2_), channel_id=1, source_target_pairs={{0,4},{1,3},{2,6},{3,1},{4,0},{5,7},{6,2},{7,5},{8,12},{9,11},{10,... | collective-permute-start | bytes 1216520 | tf_op jit(solution)/shard_map/ppermute | solution.py:37
  54.8 20.2 %collective-permute-start.16 = (bf16[48,4224]{1,0:T(8,128)(2,1)S(1)}, bf16[48,4224]{1,0:T(8,128)(2,1)S(1)}, u32[]{:S(2)}, u32[]{:S(2)}) collective-permute-start(bf16[48,4224]{1,0:T(8,128)(2,1)S(1)} %collective-permute-done.14.refs_1_), channel_id=1, source_target_pairs={{0,4},{1,3},{2,6},{3,1},{4,0},{5,7},{6,2},{7,5},{8,12},{9,11},{10,... | collective-permute-start | bytes 1216520 | tf_op jit(solution)/shard_map/ppermute | solution.py:37
  56.3 18.7 %collective-permute-start.17 = (bf16[48,4224]{1,0:T(8,128)(2,1)S(1)}, bf16[48,4224]{1,0:T(8,128)(2,1)S(1)}, u32[]{:S(2)}, u32[]{:S(2)}) collective-permute-start(bf16[48,4224]{1,0:T(8,128)(2,1)S(1)} %collective-permute-done.15.refs_2_), channel_id=1, source_target_pairs={{0,4},{1,3},{2,6},{3,1},{4,0},{5,7},{6,2},{7,5},{8,12},{9,11},{10,... | collective-permute-start | bytes 1216520 | tf_op jit(solution)/shard_map/ppermute | solution.py:37
  64.9 18.2 %collective-permute-start.23 = (bf16[48,4224]{1,0:T(8,128)(2,1)S(1)}, bf16[48,4224]{1,0:T(8,128)(2,1)S(1)}, u32[]{:S(2)}, u32[]{:S(2)}) collective-permute-start(bf16[48,4224]{1,0:T(8,128)(2,1)S(1)} %collective-permute-done.21.refs_1_), channel_id=1, source_target_pairs={{0,4},{1,3},{2,6},{3,1},{4,0},{5,7},{6,2},{7,5},{8,12},{9,11},{10,... | collective-permute-start | bytes 1216520 | tf_op jit(solution)/shard_map/ppermute | solution.py:37
  66.4 16.6 %collective-permute-start.24 = (bf16[48,4224]{1,0:T(8,128)(2,1)S(1)}, bf16[48,4224]{1,0:T(8,128)(2,1)S(1)}, u32[]{:S(2)}, u32[]{:S(2)}) collective-permute-start(bf16[48,4224]{1,0:T(8,128)(2,1)S(1)} %collective-permute-done.22.refs_2_), channel_id=1, source_target_pairs={{0,4},{1,3},{2,6},{3,1},{4,0},{5,7},{6,2},{7,5},{8,12},{9,11},{10,... | collective-permute-start | bytes 1216520 | tf_op jit(solution)/shard_map/ppermute | solution.py:37
  92.7 53.6 %collective-permute-start.30 = (bf16[384,2048]{1,0:T(8,128)(2,1)S(1)}, bf16[384,2048]{1,0:T(8,128)(2,1)S(1)}, u32[]{:S(2)}, u32[]{:S(2)}) collective-permute-start(bf16[384,2048]{1,0:T(8,128)(2,1)S(1)} %convolution_convert_fusion), channel_id=1, source_target_pairs={{0,1},{1,0},{2,3},{3,2},{4,5},{5,4},{6,7},{7,6},{8,9},{9,8},{10,11... | collective-permute-start | bytes 4718600 | tf_op jit(solution)/shard_map/ppermute | solution.py:37
  92.8 7.8 %collective-permute-start.11 = (bf16[96,2048]{1,0:T(8,128)(2,1)S(1)}, bf16[96,2048]{1,0:T(8,128)(2,1)S(1)}, u32[]{:S(2)}, u32[]{:S(2)}) collective-permute-start(bf16[96,2048]{1,0:T(8,128)(2,1)S(1)} %get-tuple-element.40), channel_id=1, source_target_pairs={{0,4},{1,3},{2,6},{3,1},{4,0},{5,7},{6,2},{7,5},{8,12},{9,11},{10,... | collective-permute-start | bytes 1179656 | tf_op jit(solution)/shard_map/ppermute | solution.py:37
  96.3 52.7 %collective-permute-start.29 = (bf16[2048,384]{1,0:T(8,128)(2,1)S(1)}, bf16[2048,384]{1,0:T(8,128)(2,1)S(1)}, u32[]{:S(2)}, u32[]{:S(2)}) collective-permute-start(bf16[2048,384]{1,0:T(8,128)(2,1)S(1)} %convolution_convert_fusion.1), channel_id=1, source_target_pairs={{0,1},{1,0},{2,3},{3,2},{4,5},{5,4},{6,7},{7,6},{8,9},{9,8},{10,11... | collective-permute-start | bytes 4718600 | tf_op jit(solution)/shard_map/ppermute | solution.py:37
  96.3 8.5 %collective-permute-start.18 = (bf16[96,2048]{1,0:T(8,128)(2,1)S(1)}, bf16[96,2048]{1,0:T(8,128)(2,1)S(1)}, u32[]{:S(2)}, u32[]{:S(2)}) collective-permute-start(bf16[96,2048]{1,0:T(8,128)(2,1)S(1)} %get-tuple-element.47), channel_id=1, source_target_pairs={{0,4},{1,3},{2,6},{3,1},{4,0},{5,7},{6,2},{7,5},{8,12},{9,11},{10,... | collective-permute-start | bytes 1179656 | tf_op jit(solution)/shard_map/ppermute | solution.py:37
  97.0 14.1 %collective-permute-start.25 = (bf16[96,2048]{1,0:T(8,128)(2,1)S(1)}, bf16[96,2048]{1,0:T(8,128)(2,1)S(1)}, u32[]{:S(2)}, u32[]{:S(2)}) collective-permute-start(bf16[96,2048]{1,0:T(8,128)(2,1)S(1)} %get-tuple-element.54), channel_id=1, source_target_pairs={{0,4},{1,3},{2,6},{3,1},{4,0},{5,7},{6,2},{7,5},{8,12},{9,11},{10,... | collective-permute-start | bytes 1179656 | tf_op jit(solution)/shard_map/ppermute | solution.py:37
  100.6 16.9 %collective-permute-start.5 = (bf16[96,2048]{1,0:T(8,128)(2,1)S(1)}, bf16[96,2048]{1,0:T(8,128)(2,1)S(1)}, u32[]{:S(2)}, u32[]{:S(2)}) collective-permute-start(bf16[96,2048]{1,0:T(8,128)(2,1)S(1)} %get-tuple-element.33), channel_id=1, source_target_pairs={{0,4},{1,3},{2,6},{3,1},{4,0},{5,7},{6,2},{7,5},{8,12},{9,11},{10,... | collective-permute-start | bytes 1179656 | tf_op jit(solution)/shard_map/ppermute | solution.py:37
  104.8 14.1 %collective-permute-start.12 = (bf16[48,2048]{1,0:T(8,128)(2,1)S(1)}, bf16[48,2048]{1,0:T(8,128)(2,1)S(1)}, u32[]{:S(2)}, u32[]{:S(2)}) collective-permute-start(bf16[48,2048]{1,0:T(8,128)(2,1)S(1)} %slice.116), channel_id=1, source_target_pairs={{0,2},{1,5},{2,0},{3,7},{4,6},{5,1},{6,4},{7,3},{8,10},{9,13},{10,... | collective-permute-start | bytes 589832 | tf_op jit(solution)/shard_map/ppermute | solution.py:37
  111.1 8.7 %collective-permute-start.19 = (bf16[48,2048]{1,0:T(8,128)(2,1)S(1)}, bf16[48,2048]{1,0:T(8,128)(2,1)S(1)}, u32[]{:S(2)}, u32[]{:S(2)}) collective-permute-start(bf16[48,2048]{1,0:T(8,128)(2,1)S(1)} %slice.115), channel_id=1, source_target_pairs={{0,2},{1,5},{2,0},{3,7},{4,6},{5,1},{6,4},{7,3},{8,10},{9,13},{10,... | collective-permute-start | bytes 589832 | tf_op jit(solution)/shard_map/ppermute | solution.py:37
  117.5 13.2 %collective-permute-start.26 = (bf16[48,2048]{1,0:T(8,128)(2,1)S(1)}, bf16[48,2048]{1,0:T(8,128)(2,1)S(1)}, u32[]{:S(2)}, u32[]{:S(2)}) collective-permute-start(bf16[48,2048]{1,0:T(8,128)(2,1)S(1)} %slice.114), channel_id=1, source_target_pairs={{0,2},{1,5},{2,0},{3,7},{4,6},{5,1},{6,4},{7,3},{8,10},{9,13},{10,... | collective-permute-start | bytes 589832 | tf_op jit(solution)/shard_map/ppermute | solution.py:37
  118.9 11.9 %collective-permute-start.6 = (bf16[48,2048]{1,0:T(8,128)(2,1)S(1)}, bf16[48,2048]{1,0:T(8,128)(2,1)S(1)}, u32[]{:S(2)}, u32[]{:S(2)}) collective-permute-start(bf16[48,2048]{1,0:T(8,128)(2,1)S(1)} %slice.117), channel_id=1, source_target_pairs={{0,2},{1,5},{2,0},{3,7},{4,6},{5,1},{6,4},{7,3},{8,10},{9,13},{10,... | collective-permute-start | bytes 589832 | tf_op jit(solution)/shard_map/ppermute | solution.py:37
  119.8 16.8 %collective-permute-start.13 = (bf16[48,2048]{1,0:T(8,128)(2,1)S(1)}, bf16[48,2048]{1,0:T(8,128)(2,1)S(1)}, u32[]{:S(2)}, u32[]{:S(2)}) collective-permute-start(bf16[48,2048]{1,0:T(8,128)(2,1)S(1)} %fusion.17), channel_id=1, source_target_pairs={{0,24},{1,25},{2,26},{3,27},{4,28},{5,29},{6,30},{7,31},{8,0},{9,1... | collective-permute-start | bytes 589832 | tf_op jit(solution)/shard_map/ppermute | solution.py:37
  130.7 14.9 %collective-permute-start.20 = (bf16[48,2048]{1,0:T(8,128)(2,1)S(1)}, bf16[48,2048]{1,0:T(8,128)(2,1)S(1)}, u32[]{:S(2)}, u32[]{:S(2)}) collective-permute-start(bf16[48,2048]{1,0:T(8,128)(2,1)S(1)} %fusion.16), channel_id=1, source_target_pairs={{0,16},{1,17},{2,18},{3,19},{4,20},{5,21},{6,22},{7,23},{8,24},{9,... | collective-permute-start | bytes 589832 | tf_op jit(solution)/shard_map/ppermute | solution.py:37
  130.8 14.7 %collective-permute-start.27 = (bf16[48,2048]{1,0:T(8,128)(2,1)S(1)}, bf16[48,2048]{1,0:T(8,128)(2,1)S(1)}, u32[]{:S(2)}, u32[]{:S(2)}) collective-permute-start(bf16[48,2048]{1,0:T(8,128)(2,1)S(1)} %fusion.15), channel_id=1, source_target_pairs={{0,8},{1,9},{2,10},{3,11},{4,12},{5,13},{6,14},{7,15},{8,16},{9,17... | collective-permute-start | bytes 589832 | tf_op jit(solution)/shard_map/ppermute | solution.py:37
  136.5 15.5 %collective-permute-start.28 = (bf16[2048,384]{1,0:T(8,128)(2,1)S(1)}, bf16[2048,384]{1,0:T(8,128)(2,1)S(1)}, u32[]{:S(2)}, u32[]{:S(2)}) collective-permute-start(bf16[2048,384]{1,0:T(8,128)(2,1)S(1)} %convolution_convert_fusion.2), channel_id=1, source_target_pairs={{0,1},{1,0},{2,3},{3,2},{4,5},{5,4},{6,7},{7,6},{8,9},{9,8},{10,11... | collective-permute-start | bytes 4718600 | tf_op jit(solution)/shard_map/ppermute | solution.py:37
